TPU v7x, 128 devices: a whole 4x4x4 slice. The times are simulated.
128 devices in a mesh: gx: 4 (over x), yz: 32 (over y, z, core).
Axes of the slice: x: 4, y: 4, z: 4, core: 2. Of those that a mesh axis runs over, the one named last changes fastest.
Arguments:
- fields: bfloat16 [24576, 5, 512], P(('gx', 'yz')), may hold values from -6 to 6
- solver_counts: int32 [128], replicated, may hold values from 16 to 192, as said below
- cnn_owner: int32 [8192], replicated, may hold values from 0 to 127, as said below
- in_weight: bfloat16 [32, 5], replicated, may hold values from -2.5 to 2.5
- in_bias: float32 [32], replicated, may hold values from -3 to 3
- depth_weight: float32 [32, 27], replicated, may hold values from -1.25 to 1.25
- depth_bias: float32 [32], replicated, may hold values from -3 to 3
- mix_weight: bfloat16 [32, 32], replicated, may hold values from -1 to 1
- mix_bias: float32 [32], replicated, may hold values from -3 to 3
- out_weight: bfloat16 [6, 32], replicated, may hold values from -1 to 1
- out_bias: float32 [6], replicated, may hold values from -3 to 3
Outputs:
- closure: bfloat16 [24576, 6, 512], P(('gx', 'yz'))
Inputs may be any that keep to these rules, and one draw needn't show every extreme that they name: Solver owner e holds its patches in slots 0 to solver_counts[e] - 1; the counts sum to 8192 and each is a multiple of a quarter of 64. `cnn_owner`: every network owner receives exactly 64 patches, and at most 2 from one solver owner.
All inputs are finite; a program needn't handle non-finite values.
Results may differ from a plain program's by a relative error of at most 0.0067.
Values may be sent and summed in bfloat16 or wider, within the bound.
A program may use at most 192 MiB of HBM per device.

v0:
```python
import jax
import jax.numpy as jnp
from jax import lax
from jax.experimental import pallas as pl
from jax.experimental.pallas import tpu as pltpu
from jax.sharding import PartitionSpec as P

MESH = pl.DeviceIdType.MESH
NDEV = 128
N_GX = 4
N_YZ = 32
CAP = 192
CIN = 5
HID = 32
COUT = 6
LANES = 128
SLOTS = 2 * NDEV
ROWS = 4 * SLOTS
F32 = jnp.float32
BF16 = jnp.bfloat16
I32 = jnp.int32
GELU_A = 2.0 * 0.7978845608028654
GELU_B = 8.0 * 0.7978845608028654 * 0.044715


def iota(shape, dim):
    return lax.broadcasted_iota(I32, shape, dim)


def dot(a, b):
    return jnp.dot(a, b, preferred_element_type=F32)


def one_hot(condition):
    return jnp.where(condition, 1.0, 0.0).astype(BF16)


def row_to_col(row):
    count = row.shape[1]
    same = iota((count, count), 0) == iota((count, count), 1)
    return jnp.sum(jnp.where(same, row, 0.0), axis=1, keepdims=True)


def col_to_row(col):
    count = col.shape[0]
    same = iota((count, count), 0) == iota((count, count), 1)
    return jnp.sum(jnp.where(same, col, 0.0), axis=0, keepdims=True)


def gelu_half(y):
    return y + y * jnp.tanh(y * (GELU_A + GELU_B * (y * y)))


def run_cumulative(me, counts, owner):
    lower = iota((NDEV, NDEV), 1) <= iota((NDEV, NDEV), 0)
    run_end = jnp.sum(jnp.where(lower, counts, 0.0), axis=1, keepdims=True).astype(I32)
    mine = one_hot(owner == me)
    rows = iota((NDEV, 64), 1)
    whole = dot(one_hot(rows < (run_end >> 7)), mine)
    part = dot(one_hot(rows == (run_end >> 7)), mine)
    inside = iota((NDEV, LANES), 1) < (run_end & 127)
    return jnp.sum(whole + jnp.where(inside, part, 0.0), axis=1, keepdims=True)


def brick_keys(cum_col):
    cum_row = col_to_row(cum_col)
    row = iota((2 * LANES, NDEV), 0)
    patch = (row & 63).astype(F32)
    below = cum_row <= patch
    source = jnp.sum(jnp.where(below, 1.0, 0.0), axis=1, keepdims=True)
    before = jnp.max(jnp.where(below, cum_row, 0.0), axis=1, keepdims=True)
    place = 2.0 * source + ((iota((2 * LANES, 1), 0) & 63).astype(F32) - before)
    row = iota((2 * LANES, 1), 0)
    key_col = 4 * place.astype(I32) + 2 * ((row >> 6) & 1) + (row >> 7)
    lane = iota((NDEV, 2 * LANES), 1)
    patch = (lane & 63).astype(F32)
    below = cum_col <= patch
    source = jnp.sum(jnp.where(below, 1.0, 0.0), axis=0, keepdims=True)
    before = jnp.max(jnp.where(below, cum_col, 0.0), axis=0, keepdims=True)
    lane = iota((1, 2 * LANES), 1)
    place = 2.0 * source + ((lane & 63).astype(F32) - before)
    key_row = 4 * place.astype(I32) + 2 * ((lane >> 6) & 1) + (lane >> 7)
    return key_col, key_row


def slot_keys(me, counts, owner):
    lane = iota((1, NDEV), 1)
    start = jnp.sum(jnp.where(lane < me, counts, 0.0), axis=1, keepdims=True).astype(I32)
    count = jnp.sum(jnp.where(lane == me, counts, 0.0), axis=1, keepdims=True).astype(I32)
    position = iota((CAP, 1), 0) + start
    rows = dot(one_hot(iota((CAP, 64), 1) == (position >> 7)), owner.astype(F32).astype(BF16))
    here = iota((CAP, LANES), 1) == (position & 127)
    owner_col = jnp.sum(jnp.where(here, rows, 0.0), axis=1, keepdims=True)
    owner_row = col_to_row(owner_col)
    same = owner_col == owner_row
    first = iota((CAP, CAP), 0)
    second = iota((CAP, CAP), 1)
    rank_col = jnp.sum(jnp.where(same & (second < first), 1.0, 0.0), axis=1, keepdims=True)
    rank_row = jnp.sum(jnp.where(same & (first < second), 1.0, 0.0), axis=0, keepdims=True)
    key_col = (2.0 * owner_col + rank_col).astype(I32)
    key_row = (2.0 * owner_row + rank_row).astype(I32)
    key_col = jnp.where(iota((CAP, 1), 0) < count, key_col, -1)
    key_row = jnp.where(iota((1, CAP), 1) < count, key_row, -1)
    return key_col, key_row


def split3(value):
    high = value.astype(BF16).astype(F32)
    middle = (value - high).astype(BF16).astype(F32)
    low = value - high - middle
    return high, middle, low


def with_bias(weight, bias_col, width):
    rows, depth = weight.shape
    tail = iota((rows, width - depth), 1)
    high, middle, low = split3(bias_col)
    extra = jnp.where(tail == 0, high, jnp.where(tail == 1, middle, jnp.where(tail == 2, low, 0.0)))
    return jnp.concatenate([weight, extra], axis=1).astype(BF16)


def move_body(
    counts_ref, owner_ref, fields_ref, in_weight_ref, in_bias_ref, depth_weight_ref, depth_bias_ref,
    mix_weight_ref, mix_bias_ref, out_weight_ref, out_bias_ref,
    back_ref, key_ref,
    spread, outgoing, incoming, grid_in, ones_mask, hidden, taps, taps_bias, result, packed,
    x_send, x_recv, y_send, y_recv, c_send, c_recv, leaving,
    send_sem, recv_sem, halo_send, halo_recv, back_send, back_recv,
):
    gx = lax.axis_index("gx")
    yz = lax.axis_index("yz")
    me = gx * N_YZ + yz

    def coords(step):
        other = lax.rem(me + step, NDEV)
        return other, (lax.div(other, N_YZ), lax.rem(other, N_YZ))

    barrier = pltpu.get_barrier_semaphore()

    def greet(step, carry):
        _, where = coords(step)
        pl.semaphore_signal(barrier, inc=1, device_id=where, device_id_type=MESH)
        return carry

    lax.fori_loop(1, NDEV, greet, 0)

    counts = counts_ref[...].astype(F32)
    owner = owner_ref[...]
    key_col, key_row = slot_keys(me, counts, owner)
    key_ref[...] = jnp.broadcast_to(key_col, (CAP, LANES))
    select = one_hot(iota((SLOTS, CAP), 0) == key_row)
    for c in range(CIN):
        rows = dot(select, fields_ref[c])
        for part in range(4):
            spread[c, pl.ds(part, SLOTS, stride=4), :] = rows[:, part * LANES : (part + 1) * LANES]
    for c in range(CIN):
        outgoing[:, :, c * LANES : (c + 1) * LANES] = (
            spread[c].reshape(NDEV, 8, LANES).astype(BF16)
        )

    pl.semaphore_wait(barrier, NDEV - 1)

    def send_out(step, carry):
        other, where = coords(step)
        pltpu.make_async_remote_copy(
            src_ref=outgoing.at[other], dst_ref=incoming.at[me],
            send_sem=send_sem, recv_sem=recv_sem, device_id=where, device_id_type=MESH,
        ).start()
        return carry

    lax.fori_loop(1, NDEV, send_out, 0)
    incoming[me] = outgoing[me]

    cum_col = run_cumulative(me, counts, owner)
    brick_col, brick_row = brick_keys(cum_col)
    gather = one_hot(iota((2 * LANES, ROWS), 1) == brick_col)
    lane = iota((1, LANES), 1)
    high_x = ((lane >> 6) & 1) == 1
    along_y = (lane >> 4) & 3
    along_z = lane & 15
    keep_low = jnp.where(gx > 0, 1.0, 0.0).astype(F32)
    keep_high = jnp.where(gx < N_GX - 1, 1.0, 0.0).astype(F32)
    for x in range(6):
        mask = jnp.ones((1, LANES), F32)
        if x == 0:
            mask = jnp.where(high_x, 1.0, keep_low)
        if x == 5:
            mask = jnp.where(high_x, keep_high, 1.0)
        ones_mask[x] = jnp.broadcast_to(mask, (16, LANES))
    depth_weight = depth_weight_ref[...]
    for tap in range(27):
        taps[tap] = jnp.broadcast_to(depth_weight[:, tap : tap + 1], (HID, LANES))
    taps_bias[...] = jnp.broadcast_to(row_to_col(depth_bias_ref[...]), (HID, LANES))
    in_weight = in_weight_ref[...].astype(F32)
    in_cols = [row_to_col(in_weight[c : c + 1, :]) for c in range(CIN)]
    column = iota((HID, 80), 1)
    base = jnp.zeros((HID, 80), F32)
    for c in range(CIN):
        base = jnp.where((column >> 4) == c, 0.5 * in_cols[c], base)
    in_bias = 0.5 * row_to_col(in_bias_ref[...])
    first_w = jnp.concatenate(
        [with_bias(jnp.where((column & 15) == cell, base, 0.0), in_bias, 96) for cell in range(16)],
        axis=0,
    )
    mix_w = with_bias(0.5 * mix_weight_ref[...].astype(F32), 0.5 * row_to_col(mix_bias_ref[...]), 48)
    out_w = with_bias(out_weight_ref[...].astype(F32), row_to_col(out_bias_ref[...]), 48)
    ones_cells = jnp.ones((16, 8 * LANES), BF16)

    every = pltpu.make_async_copy(
        outgoing.at[pl.ds(0, NDEV - 1)], incoming.at[pl.ds(0, NDEV - 1)], recv_sem
    )
    every.wait()

    bricks = dot(gather, incoming[...].reshape(ROWS, CIN * LANES))
    for c in range(CIN):
        for m in range(2):
            turned = bricks[m * LANES : (m + 1) * LANES, c * LANES : (c + 1) * LANES].T
            for p in range(2):
                grid_in[c, pl.ds((1 + 2 * m + p) * 80 + 8, 64), :] = turned[p * 64 : (p + 1) * 64]

    for c in range(CIN):
        x_send[0, c] = pltpu.roll(grid_in[c, pl.ds(4 * 80 + 8, 64), :], 64, 1).astype(BF16)
        x_send[1, c] = pltpu.roll(grid_in[c, pl.ds(1 * 80 + 8, 64), :], 64, 1).astype(BF16)
        last_y = [grid_in[c, pl.ds(x * 80 + 64, 8), :] for x in range(1, 5)]
        first_y = [grid_in[c, pl.ds(x * 80 + 8, 8), :] for x in range(1, 5)]
        y_send[0, c] = pltpu.roll(jnp.concatenate(last_y, axis=0), 80, 1).astype(BF16)
        y_send[1, c] = pltpu.roll(jnp.concatenate(first_y, axis=0), 48, 1).astype(BF16)
        c_send[0, c] = pltpu.roll(last_y[3], 16, 1).astype(BF16)
        c_send[1, c] = pltpu.roll(first_y[3], 112, 1).astype(BF16)
        c_send[2, c] = pltpu.roll(last_y[0], 16, 1).astype(BF16)
        c_send[3, c] = pltpu.roll(first_y[0], 112, 1).astype(BF16)
    up_x = lax.rem(gx + 1, N_GX)
    down_x = lax.rem(gx + N_GX - 1, N_GX)
    up_y = lax.rem(yz + 1, N_YZ)
    down_y = lax.rem(yz + N_YZ - 1, N_YZ)
    halo = []
    for source, target, where in (
        (x_send.at[0], x_recv.at[0], (up_x, yz)),
        (x_send.at[1], x_recv.at[1], (down_x, yz)),
        (y_send.at[0], y_recv.at[0], (gx, up_y)),
        (y_send.at[1], y_recv.at[1], (gx, down_y)),
        (c_send.at[0], c_recv.at[0], (up_x, up_y)),
        (c_send.at[1], c_recv.at[1], (up_x, down_y)),
        (c_send.at[2], c_recv.at[2], (down_x, up_y)),
        (c_send.at[3], c_recv.at[3], (down_x, down_y)),
    ):
        number = len(halo)
        copy = pltpu.make_async_remote_copy(
            src_ref=source, dst_ref=target, send_sem=halo_send.at[number],
            recv_sem=halo_recv.at[number], device_id=where, device_id_type=MESH,
        )
        copy.start()
        halo.append(copy)
    for copy in halo:
        copy.wait()

    for c in range(CIN):
        low = jnp.where(high_x, x_send[0, c].astype(F32), keep_low * x_recv[0, c].astype(F32))
        high = jnp.where(high_x, keep_high * x_recv[1, c].astype(F32), x_send[1, c].astype(F32))
        grid_in[c, pl.ds(8, 64), :] = low
        grid_in[c, pl.ds(5 * 80 + 8, 64), :] = high
        for side in range(2):
            own = y_recv[side, c].astype(F32)
            corner_low = keep_low * c_recv[0 + side, c].astype(F32)
            corner_high = keep_high * c_recv[2 + side, c].astype(F32)
            edge_lane = along_y == (0 if side == 0 else 3)
            for x in range(6):
                if x == 0:
                    far = jnp.where(high_x, pltpu.roll(own[24:32], 64, 1), corner_low)
                elif x == 5:
                    far = jnp.where(high_x, corner_high, pltpu.roll(own[0:8], 64, 1))
                else:
                    far = own[8 * (x - 1) : 8 * x]
                near = grid_in[c, pl.ds(x * 80 + (64 if side == 0 else 8), 8), :]
                near = pltpu.roll(near, 16 if side == 0 else 112, 1)
                grid_in[c, pl.ds(x * 80 + (0 if side == 0 else 72), 8), :] = jnp.where(
                    edge_lane, far, near
                )

    def first_group(group, carry):
        x = lax.div(group, 5)
        pair = lax.rem(group, 5)
        start = pl.multiple_of(group * 16, 16)
        cells = [grid_in[c, pl.ds(start, 16), :] for c in range(CIN)]
        stacked = jnp.concatenate(cells + [ones_mask[x]], axis=0).astype(BF16)
        value = gelu_half(dot(first_w, stacked)).astype(BF16).astype(F32)
        for cell in range(16):
            y = 2 * pair + cell // 8
            z = cell % 8
            here = value[cell * HID : (cell + 1) * HID]
            hidden[x, y, 1 + z] = here
            if z == 7:
                hidden[x, y, 0] = jnp.where(
                    along_z == 0, pltpu.roll(here, 113, 1), pltpu.roll(here, 1, 1)
                )
            if z == 0:
                hidden[x, y, 9] = jnp.where(
                    along_z == 15, pltpu.roll(here, 15, 1), pltpu.roll(here, 127, 1)
                )
        return carry

    lax.fori_loop(0, 30, first_group, 0)

    def depth_group(group, carry):
        x = lax.div(group, 8)
        y = lax.rem(group, 8)
        columns = [[] for _ in range(8)]
        for part in range(4):
            rows = pl.ds(8 * part, 8)
            total = [taps_bias[rows, :]] * 8
            for a in range(3):
                for b in range(3):
                    cells = [hidden[x + a, y + b, z, rows, :] for z in range(10)]
                    for c in range(3):
                        weight = taps[9 * a + 3 * b + c, rows, :]
                        for z in range(8):
                            total[z] = total[z] + weight * cells[z + c]
            for z in range(8):
                columns[z].append(total[z])
        depth = jnp.concatenate(
            [jnp.concatenate(column, axis=0).astype(BF16) for column in columns], axis=1
        )
        mixed = gelu_half(dot(mix_w, jnp.concatenate([depth, ones_cells], axis=0))).astype(BF16)
        field = dot(out_w, jnp.concatenate([mixed, ones_cells], axis=0))
        for z in range(8):
            start = pl.multiple_of(group * 64 + 8 * z, 8)
            result[pl.ds(start, COUT), :] = field[:, z * LANES : (z + 1) * LANES]
        return carry

    lax.fori_loop(0, 32, depth_group, 0)

    for f in range(COUT):
        for m in range(2):
            cells = result[pl.ds(m * 1024 + f, LANES, stride=8), :]
            packed[m * LANES : (m + 1) * LANES, f * LANES : (f + 1) * LANES] = cells.T.astype(BF16)
    scatter = one_hot(iota((ROWS, 2 * LANES), 0) == brick_row)
    leaving[...] = dot(scatter, packed[...]).reshape(NDEV, 8, COUT * LANES).astype(BF16)

    def send_back(step, carry):
        other, where = coords(step)
        pltpu.make_async_remote_copy(
            src_ref=leaving.at[other], dst_ref=back_ref.at[me],
            send_sem=back_send, recv_sem=back_recv, device_id=where, device_id_type=MESH,
        ).start()
        return carry

    lax.fori_loop(1, NDEV, send_back, 0)
    back_ref[me] = leaving[me]
    pltpu.make_async_copy(
        outgoing.at[pl.ds(0, NDEV - 1)], incoming.at[pl.ds(0, NDEV - 1)], send_sem
    ).wait()
    for semaphore in (back_send, back_recv):
        pltpu.make_async_copy(
            leaving.at[pl.ds(0, NDEV - 1)], back_ref.at[pl.ds(0, NDEV - 1)], semaphore
        ).wait()


def unpack_body(back_ref, key_ref, out_ref):
    key = key_ref[...][:, :1]
    rows = iota((CAP, ROWS), 1)
    arrived = back_ref[...].reshape(ROWS, COUT * LANES)
    for part in range(4):
        wanted = jnp.where(key < 0, -1, 4 * key + part)
        taken = dot(one_hot(rows == wanted), arrived).astype(BF16)
        for f in range(COUT):
            out_ref[f, :, part * LANES : (part + 1) * LANES] = taken[:, f * LANES : (f + 1) * LANES]


VMEM = pl.BlockSpec(memory_space=pltpu.VMEM)


def shards(
    fields, solver_counts, cnn_owner, in_weight, in_bias, depth_weight, depth_bias,
    mix_weight, mix_bias, out_weight, out_bias,
):
    back, key = pl.pallas_call(
        move_body,
        out_shape=(
            jax.ShapeDtypeStruct((NDEV, 8, COUT * LANES), BF16),
            jax.ShapeDtypeStruct((CAP, LANES), I32),
        ),
        in_specs=[VMEM] * 11,
        out_specs=(VMEM, VMEM),
        scratch_shapes=[
            pltpu.VMEM((CIN, ROWS, LANES), F32),
            pltpu.VMEM((NDEV, 8, CIN * LANES), BF16),
            pltpu.VMEM((NDEV, 8, CIN * LANES), BF16),
            pltpu.VMEM((CIN, 480, LANES), F32),
            pltpu.VMEM((6, 16, LANES), F32),
            pltpu.VMEM((6, 10, 10, HID, LANES), F32),
            pltpu.VMEM((27, HID, LANES), F32),
            pltpu.VMEM((HID, LANES), F32),
            pltpu.VMEM((2048, LANES), F32),
            pltpu.VMEM((2 * LANES, COUT * LANES), BF16),
            pltpu.VMEM((2, CIN, 64, LANES), BF16),
            pltpu.VMEM((2, CIN, 64, LANES), BF16),
            pltpu.VMEM((2, CIN, 32, LANES), BF16),
            pltpu.VMEM((2, CIN, 32, LANES), BF16),
            pltpu.VMEM((4, CIN, 8, LANES), BF16),
            pltpu.VMEM((4, CIN, 8, LANES), BF16),
            pltpu.VMEM((NDEV, 8, COUT * LANES), BF16),
            pltpu.SemaphoreType.DMA,
            pltpu.SemaphoreType.DMA,
            pltpu.SemaphoreType.DMA((8,)),
            pltpu.SemaphoreType.DMA((8,)),
            pltpu.SemaphoreType.DMA,
            pltpu.SemaphoreType.DMA,
        ],
        compiler_params=pltpu.CompilerParams(
            collective_id=0, has_side_effects=True, vmem_limit_bytes=60 * 1024 * 1024
        ),
        name="closure",
    )(
        solver_counts.reshape(1, NDEV),
        cnn_owner.reshape(64, LANES),
        jnp.transpose(fields, (1, 0, 2)),
        jnp.transpose(in_weight),
        in_bias.reshape(1, HID),
        depth_weight,
        depth_bias.reshape(1, HID),
        mix_weight,
        mix_bias.reshape(1, HID),
        out_weight,
        out_bias.reshape(1, COUT),
    )
    closure = pl.pallas_call(
        unpack_body,
        out_shape=jax.ShapeDtypeStruct((COUT, CAP, 4 * LANES), BF16),
        in_specs=[VMEM] * 2,
        out_specs=VMEM,
        compiler_params=pltpu.CompilerParams(vmem_limit_bytes=60 * 1024 * 1024),
        name="unpack",
    )(back, key)
    return jnp.transpose(closure, (1, 0, 2))


def solution(mesh):
    return jax.shard_map(
        shards,
        mesh=mesh,
        in_specs=(P(("gx", "yz"), None, None), P(), P(), P(), P(), P(), P(), P(), P(), P(), P()),
        out_specs=P(("gx", "yz"), None, None),
        check_vma=False,
    )
```

profile of v0, /device:TPU:25, one launch (start us, length us, event | category | flops | bytes accessed | tf_op | source)
XLA Modules:
  0.0 107.1 jit_solution(14981562978214460090)
XLA Ops:
  0.0 103.2 %closure.1 = (bf16[128,8,768]{2,1,0:T(8,128)(2,1)}, s32[192,128]{1,0:T(8,128)}) custom-call(s32[1,128]{1,0:T(1,128)} %bitcast.12, s32[64,128]{1,0:T(8,128)} %bitcast.10, bf16[5,192,512]{2,1,0:T(8,128)(2,1)} %bitcast.9, bf16[5,32]{1,0:T(8,128)(2,1)} %bitcast.11, f32[1,32]{1,0:T(1,128)} %bitcast.13, f32[32,27]{1,0:T(8,128)} %depth_weight_ref.1, ...), custom_call_target="tpu_custom_call" | custom-call | tf_op jit(solution)/shard_map/closure/pallas_call | solution.py:376
  103.2 3.9 %unpack.1 = bf16[6,192,512]{2,1,0:T(8,128)(2,1)} custom-call(bf16[128,8,768]{2,1,0:T(8,128)(2,1)} %get-tuple-element.7.back_ref, s32[192,128]{1,0:T(8,128)} %get-tuple-element.8.key_ref), custom_call_target="tpu_custom_call" | custom-call | tf_op jit(solution)/shard_map/unpack/pallas_call | solution.py:426
where the time goes:
time: 107 us
  Pallas kernels  107 us (100%)
    pallas_call x1, Pallas kernels, shards(): pl.pallas_call(move_body, out_shape=(jax.ShapeDtypeStruct((NDEV, 8, COUT...  103 us
    pallas_call x1, Pallas kernels, shards(): pl.pallas_call(unpack_body, out_shape=jax.ShapeDtypeStruct((COUT, CAP, 4...  3.92 us

commit v1 on v0

--- a/solution.py
+++ b/solution.py
@@ -23,6 +23,12 @@
 GELU_B = 8.0 * 0.7978845608028654 * 0.044715
 
 
+STEPS = sorted(
+    [(x, y, z, c) for x in range(4) for y in range(4) for z in range(4) for c in range(2)],
+    key=lambda step: -sum(min(part, 4 - part) for part in step[:3]),
+)[:-2] + [(0, 0, 0, 1)]
+
+
 def iota(shape, dim):
     return lax.broadcasted_iota(I32, shape, dim)
 
@@ -69,17 +75,16 @@
     below = cum_row <= patch
     source = jnp.sum(jnp.where(below, 1.0, 0.0), axis=1, keepdims=True)
     before = jnp.max(jnp.where(below, cum_row, 0.0), axis=1, keepdims=True)
-    place = 2.0 * source + ((iota((2 * LANES, 1), 0) & 63).astype(F32) - before)
     row = iota((2 * LANES, 1), 0)
+    place = 2.0 * source + ((row & 63).astype(F32) - before)
     key_col = 4 * place.astype(I32) + 2 * ((row >> 6) & 1) + (row >> 7)
-    lane = iota((NDEV, 2 * LANES), 1)
-    patch = (lane & 63).astype(F32)
+    patch = (iota((NDEV, LANES), 1) & 63).astype(F32)
     below = cum_col <= patch
     source = jnp.sum(jnp.where(below, 1.0, 0.0), axis=0, keepdims=True)
     before = jnp.max(jnp.where(below, cum_col, 0.0), axis=0, keepdims=True)
-    lane = iota((1, 2 * LANES), 1)
+    lane = iota((1, LANES), 1)
     place = 2.0 * source + ((lane & 63).astype(F32) - before)
-    key_row = 4 * place.astype(I32) + 2 * ((lane >> 6) & 1) + (lane >> 7)
+    key_row = 2 * place.astype(I32) + (lane >> 6)
     return key_col, key_row
 
 
@@ -119,35 +124,33 @@
     return jnp.concatenate([weight, extra], axis=1).astype(BF16)
 
 
-def move_body(
+def closure_body(
     counts_ref, owner_ref, fields_ref, in_weight_ref, in_bias_ref, depth_weight_ref, depth_bias_ref,
     mix_weight_ref, mix_bias_ref, out_weight_ref, out_bias_ref,
-    back_ref, key_ref,
-    spread, outgoing, incoming, grid_in, ones_mask, hidden, taps, taps_bias, result, packed,
-    x_send, x_recv, y_send, y_recv, c_send, c_recv, leaving,
+    out_ref,
+    spread, outgoing, incoming, grid_in, ones_mask, hidden, taps, taps_bias, depth, result, scatter,
+    place_slots, x_send, x_recv, y_send, y_recv, c_send, c_recv, leaving, arrived,
     send_sem, recv_sem, halo_send, halo_recv, back_send, back_recv,
 ):
     gx = lax.axis_index("gx")
     yz = lax.axis_index("yz")
     me = gx * N_YZ + yz
+    at_x = [lax.rem(gx + step, 4) for step in range(4)]
+    at_y = [8 * lax.rem(lax.div(yz, 8) + step, 4) for step in range(4)]
+    at_z = [2 * lax.rem(lax.div(yz, 2) + step, 4) for step in range(4)]
+    at_core = [lax.rem(yz + step, 2) for step in range(2)]
 
     def coords(step):
-        other = lax.rem(me + step, NDEV)
-        return other, (lax.div(other, N_YZ), lax.rem(other, N_YZ))
+        where = (at_x[step[0]], at_y[step[1]] + at_z[step[2]] + at_core[step[3]])
+        return where[0] * N_YZ + where[1], where
 
     barrier = pltpu.get_barrier_semaphore()
-
-    def greet(step, carry):
-        _, where = coords(step)
-        pl.semaphore_signal(barrier, inc=1, device_id=where, device_id_type=MESH)
-        return carry
-
-    lax.fori_loop(1, NDEV, greet, 0)
+    for step in STEPS:
+        pl.semaphore_signal(barrier, inc=1, device_id=coords(step)[1], device_id_type=MESH)
 
     counts = counts_ref[...].astype(F32)
     owner = owner_ref[...]
     key_col, key_row = slot_keys(me, counts, owner)
-    key_ref[...] = jnp.broadcast_to(key_col, (CAP, LANES))
     select = one_hot(iota((SLOTS, CAP), 0) == key_row)
     for c in range(CIN):
         rows = dot(select, fields_ref[c])
@@ -160,20 +163,23 @@
 
     pl.semaphore_wait(barrier, NDEV - 1)
 
-    def send_out(step, carry):
+    for step in STEPS:
         other, where = coords(step)
         pltpu.make_async_remote_copy(
             src_ref=outgoing.at[other], dst_ref=incoming.at[me],
             send_sem=send_sem, recv_sem=recv_sem, device_id=where, device_id_type=MESH,
         ).start()
-        return carry
-
-    lax.fori_loop(1, NDEV, send_out, 0)
     incoming[me] = outgoing[me]
 
     cum_col = run_cumulative(me, counts, owner)
     brick_col, brick_row = brick_keys(cum_col)
     gather = one_hot(iota((2 * LANES, ROWS), 1) == brick_col)
+    scatter[...] = one_hot(iota((2 * SLOTS, LANES), 0) == brick_row)
+    for half in range(2):
+        wanted = jnp.where(key_col < 0, -1, 2 * key_col + half)
+        place_slots[half * CAP : (half + 1) * CAP, :] = one_hot(
+            iota((CAP, 2 * SLOTS), 1) == wanted
+        )
     lane = iota((1, LANES), 1)
     high_x = ((lane >> 6) & 1) == 1
     along_y = (lane >> 4) & 3
@@ -251,6 +257,32 @@
         )
         copy.start()
         halo.append(copy)
+    def first_group(x, pair):
+        start = pl.multiple_of(x * 80 + pair * 16, 16)
+        cells = [grid_in[c, pl.ds(start, 16), :] for c in range(CIN)]
+        stacked = jnp.concatenate(cells + [ones_mask[x]], axis=0).astype(BF16)
+        value = gelu_half(dot(first_w, stacked)).astype(BF16).astype(F32)
+        for cell in range(16):
+            y = 2 * pair + cell // 8
+            z = cell % 8
+            here = value[cell * HID : (cell + 1) * HID]
+            hidden[x, y, 1 + z] = here
+            if z == 7:
+                hidden[x, y, 0] = jnp.where(
+                    along_z == 0, pltpu.roll(here, 113, 1), pltpu.roll(here, 1, 1)
+                )
+            if z == 0:
+                hidden[x, y, 9] = jnp.where(
+                    along_z == 15, pltpu.roll(here, 15, 1), pltpu.roll(here, 127, 1)
+                )
+
+    def first_inner(x, carry):
+        for pair in range(1, 4):
+            first_group(x, pair)
+        return carry
+
+    lax.fori_loop(1, 5, first_inner, 0)
+
     for copy in halo:
         copy.wait()
 
@@ -277,36 +309,23 @@
                     edge_lane, far, near
                 )
 
-    def first_group(group, carry):
-        x = lax.div(group, 5)
-        pair = lax.rem(group, 5)
-        start = pl.multiple_of(group * 16, 16)
-        cells = [grid_in[c, pl.ds(start, 16), :] for c in range(CIN)]
-        stacked = jnp.concatenate(cells + [ones_mask[x]], axis=0).astype(BF16)
-        value = gelu_half(dot(first_w, stacked)).astype(BF16).astype(F32)
-        for cell in range(16):
-            y = 2 * pair + cell // 8
-            z = cell % 8
-            here = value[cell * HID : (cell + 1) * HID]
-            hidden[x, y, 1 + z] = here
-            if z == 7:
-                hidden[x, y, 0] = jnp.where(
-                    along_z == 0, pltpu.roll(here, 113, 1), pltpu.roll(here, 1, 1)
-                )
-            if z == 0:
-                hidden[x, y, 9] = jnp.where(
-                    along_z == 15, pltpu.roll(here, 15, 1), pltpu.roll(here, 127, 1)
-                )
+    def first_edge_y(x, carry):
+        first_group(x, 0)
+        first_group(x, 4)
         return carry
 
-    lax.fori_loop(0, 30, first_group, 0)
-
-    def depth_group(group, carry):
-        x = lax.div(group, 8)
-        y = lax.rem(group, 8)
-        columns = [[] for _ in range(8)]
-        for part in range(4):
-            rows = pl.ds(8 * part, 8)
+    def first_edge_x(pair, carry):
+        first_group(0, pair)
+        first_group(5, pair)
+        return carry
+
+    lax.fori_loop(1, 5, first_edge_y, 0)
+    lax.fori_loop(0, 5, first_edge_x, 0)
+
+    def plane(x, carry):
+        def depth_part(group, inner):
+            y = lax.div(group, 4)
+            rows = pl.ds(pl.multiple_of(8 * lax.rem(group, 4), 8), 8)
             total = [taps_bias[rows, :]] * 8
             for a in range(3):
                 for b in range(3):
@@ -316,54 +335,67 @@
                         for z in range(8):
                             total[z] = total[z] + weight * cells[z + c]
             for z in range(8):
-                columns[z].append(total[z])
-        depth = jnp.concatenate(
-            [jnp.concatenate(column, axis=0).astype(BF16) for column in columns], axis=1
-        )
-        mixed = gelu_half(dot(mix_w, jnp.concatenate([depth, ones_cells], axis=0))).astype(BF16)
-        field = dot(out_w, jnp.concatenate([mixed, ones_cells], axis=0))
-        for z in range(8):
-            start = pl.multiple_of(group * 64 + 8 * z, 8)
-            result[pl.ds(start, COUT), :] = field[:, z * LANES : (z + 1) * LANES]
+                depth[y, z, rows, :] = total[z]
+            return inner
+
+        lax.fori_loop(0, 32, depth_part, 0)
+
+        def mix_part(y, inner):
+            columns = [depth[y, z].astype(BF16) for z in range(8)]
+            stacked = jnp.concatenate([jnp.concatenate(columns, axis=1), ones_cells], axis=0)
+            mixed = gelu_half(dot(mix_w, stacked)).astype(BF16)
+            field = dot(out_w, jnp.concatenate([mixed, ones_cells], axis=0))
+            for z in range(8):
+                start = pl.multiple_of(y * 64 + 8 * z, 8)
+                result[pl.ds(start, COUT), :] = field[:, z * LANES : (z + 1) * LANES]
+            return inner
+
+        lax.fori_loop(0, 8, mix_part, 0)
+
+        odd = lax.rem(x, 2)
+        turned = []
+        for pair in range(3):
+            first = result[pl.ds(2 * pair + odd, 64, stride=8), :]
+            second = result[pl.ds(2 * pair + 1 - odd, 64, stride=8), :]
+            turned.append(jnp.concatenate([first, second], axis=0).T.astype(BF16))
+        packed = jnp.concatenate(turned, axis=1)
+        leaving[x] = dot(scatter[...], packed).reshape(NDEV, 4, 3 * LANES).astype(BF16)
+        for step in STEPS:
+            other, where = coords(step)
+            pltpu.make_async_remote_copy(
+                src_ref=leaving.at[x, other], dst_ref=arrived.at[x, me],
+                send_sem=back_send, recv_sem=back_recv.at[x], device_id=where, device_id_type=MESH,
+            ).start()
+        arrived[x, me] = leaving[x, me]
         return carry
 
-    lax.fori_loop(0, 32, depth_group, 0)
-
-    for f in range(COUT):
-        for m in range(2):
-            cells = result[pl.ds(m * 1024 + f, LANES, stride=8), :]
-            packed[m * LANES : (m + 1) * LANES, f * LANES : (f + 1) * LANES] = cells.T.astype(BF16)
-    scatter = one_hot(iota((ROWS, 2 * LANES), 0) == brick_row)
-    leaving[...] = dot(scatter, packed[...]).reshape(NDEV, 8, COUT * LANES).astype(BF16)
-
-    def send_back(step, carry):
-        other, where = coords(step)
-        pltpu.make_async_remote_copy(
-            src_ref=leaving.at[other], dst_ref=back_ref.at[me],
-            send_sem=back_send, recv_sem=back_recv, device_id=where, device_id_type=MESH,
-        ).start()
-        return carry
-
-    lax.fori_loop(1, NDEV, send_back, 0)
-    back_ref[me] = leaving[me]
+    lax.fori_loop(0, 4, plane, 0)
+
+    low_half = iota((1, LANES), 1) < 64
+    taken = []
+    for x in range(4):
+        pltpu.make_async_copy(
+            leaving.at[x, pl.ds(0, NDEV - 1)], arrived.at[x, pl.ds(0, NDEV - 1)], back_recv.at[x]
+        ).wait()
+        taken.append(dot(place_slots[...], arrived[x].reshape(2 * SLOTS, 3 * LANES)))
+        if x % 2 == 0:
+            continue
+        for half in range(2):
+            rows = slice(half * CAP, (half + 1) * CAP)
+            lanes = slice((2 * half + x // 2) * LANES, (2 * half + x // 2 + 1) * LANES)
+            for pair in range(3):
+                even = taken[x - 1][rows, pair * LANES : (pair + 1) * LANES]
+                odd = taken[x][rows, pair * LANES : (pair + 1) * LANES]
+                out_ref[2 * pair, :, lanes] = jnp.where(low_half, even, odd).astype(BF16)
+                out_ref[2 * pair + 1, :, lanes] = pltpu.roll(
+                    jnp.where(low_half, odd, even), 64, 1
+                ).astype(BF16)
     pltpu.make_async_copy(
         outgoing.at[pl.ds(0, NDEV - 1)], incoming.at[pl.ds(0, NDEV - 1)], send_sem
     ).wait()
-    for semaphore in (back_send, back_recv):
-        pltpu.make_async_copy(
-            leaving.at[pl.ds(0, NDEV - 1)], back_ref.at[pl.ds(0, NDEV - 1)], semaphore
-        ).wait()
-
-
-def unpack_body(back_ref, key_ref, out_ref):
-    key = key_ref[...][:, :1]
-    rows = iota((CAP, ROWS), 1)
-    arrived = back_ref[...].reshape(ROWS, COUT * LANES)
-    for part in range(4):
-        wanted = jnp.where(key < 0, -1, 4 * key + part)
-        taken = dot(one_hot(rows == wanted), arrived).astype(BF16)
-        for f in range(COUT):
-            out_ref[f, :, part * LANES : (part + 1) * LANES] = taken[:, f * LANES : (f + 1) * LANES]
+    pltpu.make_async_copy(
+        leaving.at[:, pl.ds(0, NDEV - 1)], arrived.at[:, pl.ds(0, NDEV - 1)], back_send
+    ).wait()
 
 
 VMEM = pl.BlockSpec(memory_space=pltpu.VMEM)
@@ -373,14 +405,11 @@
     fields, solver_counts, cnn_owner, in_weight, in_bias, depth_weight, depth_bias,
     mix_weight, mix_bias, out_weight, out_bias,
 ):
-    back, key = pl.pallas_call(
-        move_body,
-        out_shape=(
-            jax.ShapeDtypeStruct((NDEV, 8, COUT * LANES), BF16),
-            jax.ShapeDtypeStruct((CAP, LANES), I32),
-        ),
+    closure = pl.pallas_call(
+        closure_body,
+        out_shape=jax.ShapeDtypeStruct((COUT, CAP, 4 * LANES), BF16),
         in_specs=[VMEM] * 11,
-        out_specs=(VMEM, VMEM),
+        out_specs=VMEM,
         scratch_shapes=[
             pltpu.VMEM((CIN, ROWS, LANES), F32),
             pltpu.VMEM((NDEV, 8, CIN * LANES), BF16),
@@ -390,21 +419,24 @@
             pltpu.VMEM((6, 10, 10, HID, LANES), F32),
             pltpu.VMEM((27, HID, LANES), F32),
             pltpu.VMEM((HID, LANES), F32),
-            pltpu.VMEM((2048, LANES), F32),
-            pltpu.VMEM((2 * LANES, COUT * LANES), BF16),
+            pltpu.VMEM((8, 8, HID, LANES), F32),
+            pltpu.VMEM((512, LANES), F32),
+            pltpu.VMEM((2 * SLOTS, LANES), BF16),
+            pltpu.VMEM((2 * CAP, 2 * SLOTS), BF16),
             pltpu.VMEM((2, CIN, 64, LANES), BF16),
             pltpu.VMEM((2, CIN, 64, LANES), BF16),
             pltpu.VMEM((2, CIN, 32, LANES), BF16),
             pltpu.VMEM((2, CIN, 32, LANES), BF16),
             pltpu.VMEM((4, CIN, 8, LANES), BF16),
             pltpu.VMEM((4, CIN, 8, LANES), BF16),
-            pltpu.VMEM((NDEV, 8, COUT * LANES), BF16),
+            pltpu.VMEM((4, NDEV, 4, 3 * LANES), BF16),
+            pltpu.VMEM((4, NDEV, 4, 3 * LANES), BF16),
             pltpu.SemaphoreType.DMA,
             pltpu.SemaphoreType.DMA,
             pltpu.SemaphoreType.DMA((8,)),
             pltpu.SemaphoreType.DMA((8,)),
             pltpu.SemaphoreType.DMA,
-            pltpu.SemaphoreType.DMA,
+            pltpu.SemaphoreType.DMA((4,)),
         ],
         compiler_params=pltpu.CompilerParams(
             collective_id=0, has_side_effects=True, vmem_limit_bytes=60 * 1024 * 1024
@@ -423,14 +455,6 @@
         out_weight,
         out_bias.reshape(1, COUT),
     )
-    closure = pl.pallas_call(
-        unpack_body,
-        out_shape=jax.ShapeDtypeStruct((COUT, CAP, 4 * LANES), BF16),
-        in_specs=[VMEM] * 2,
-        out_specs=VMEM,
-        compiler_params=pltpu.CompilerParams(vmem_limit_bytes=60 * 1024 * 1024),
-        name="unpack",
-    )(back, key)
     return jnp.transpose(closure, (1, 0, 2))
 
 

time: 107 us -> 74.5 us (0.70)
  the two profiles are of different devices: /device:TPU:25 before, /device:TPU:1 now
where the time goes in v1:
time: 74.5 us; the launch traced here: 74.3 us
  Pallas kernels  71.9 us (97%)
  local copies, waits for them, and re-layouts  2.42 us (3%)
    pallas_call x1, Pallas kernels, shards(): pl.pallas_call(closure_body, out_shape=jax.ShapeDtypeStruct((COUT, CAP, 4...  71.9 us
    unnamed x1, local copies, waits for them, and re-layouts  2.42 us

profile of v1, /device:TPU:1, one launch (start us, length us, event | category | flops | bytes accessed | tf_op | source)
XLA Modules:
  0.0 74.3 jit_solution(8655842765105290088)
XLA Ops:
  0.0 71.9 %closure.1 = bf16[6,192,512]{2,1,0:T(8,128)(2,1)} custom-call(s32[1,128]{1,0:T(1,128)} %bitcast.13, s32[64,128]{1,0:T(8,128)} %bitcast.11, bf16[5,192,512]{2,1,0:T(8,128)(2,1)} %bitcast.10, bf16[5,32]{1,0:T(8,128)(2,1)} %bitcast.12, f32[1,32]{1,0:T(1,128)} %bitcast.14, f32[32,27]{1,0:T(8,128)} %depth_weight_ref.1, f32[1,32]{1,0:T(1,128)} %bitcast.15, ...), custom_call_target="tpu_custom_call" | custom-call | tf_op jit(solution)/shard_map/closure/pallas_call | solution.py:408
  71.9 2.4 %copy.13 = bf16[192,6,512]{2,0,1:T(8,128)(2,1)} copy(bf16[192,6,512]{2,0,1:T(8,128)(2,1)} %bitcast.9) | data formatting | bytes 2359296

commit v2 on v1

--- a/solution.py
+++ b/solution.py
@@ -116,19 +116,61 @@
     return high, middle, low
 
 
-def with_bias(weight, bias_col, width):
+def repeat_rows(value, count):
+    rows, lanes = value.shape
+    return jnp.broadcast_to(value[:, None, :], (rows, count, lanes)).reshape(rows * count, lanes)
+
+
+def first_weights(in_weight, in_bias, z_halo):
+    lane = iota((HID, 96), 1)
+    base = jnp.zeros((HID, 96), F32)
+    for c in range(CIN):
+        base = jnp.where((lane >> 4) == c, 0.5 * row_to_col(in_weight[c : c + 1, :]), base)
+    for number, part in enumerate(split3(0.5 * row_to_col(in_bias))):
+        for mask in range(3):
+            base = jnp.where(lane == 80 + 3 * mask + number, part, base)
+    base = repeat_rows(base, 16)
+    lane = iota((16 * HID, 96), 1)
+    cell = iota((16 * HID, 96), 0) & 15
+    first = jnp.where(cell < 2, 83, jnp.where((cell >> 1) == 5, 86, 80)) if z_halo else 80
+    own = jnp.where(lane < 80, cell, -1) == (lane & 15)
+    keep = own | ((lane >= first) & (lane < first + 3))
+    return jnp.where(keep, base, 0.0).astype(BF16)
+
+
+def over_cells(weight):
     rows, depth = weight.shape
-    tail = iota((rows, width - depth), 1)
-    high, middle, low = split3(bias_col)
-    extra = jnp.where(tail == 0, high, jnp.where(tail == 1, middle, jnp.where(tail == 2, low, 0.0)))
-    return jnp.concatenate([weight, extra], axis=1).astype(BF16)
+    widen = one_hot(iota((depth, 8 * depth), 0) == (iota((depth, 8 * depth), 1) >> 3))
+    wide = repeat_rows(dot(weight, widen), 8)
+    keep = (iota(wide.shape, 0) & 7) == (iota(wide.shape, 1) & 7)
+    return jnp.where(keep, wide, 0.0).astype(BF16)
+
+
+def tap_places(x, pair):
+    lane = iota((1, 2048), 1)
+    z = lane >> 8
+    side = (lane >> 7) & 1
+    row = lane & 127
+    edge = row - 96
+    far = edge & 15
+    regular = row < 96
+    in_x = jnp.where(regular, row >> 4, far >> 1)
+    in_y = jnp.where(regular, (row >> 3) & 1, far & 1)
+    in_z = jnp.where(regular, row & 7, jnp.where(edge >= 16, 8, -1))
+    a = in_x - x
+    b = 2 * side + in_y - pair
+    c = in_z - z + 1
+    valid = (a >= 0) & (a <= 2) & (b >= 0) & (b <= 2) & (c >= 0) & (c <= 2)
+    valid = valid & (regular | (far < 12))
+    tap = jnp.where(valid, 9 * a + 3 * b + c, -1)
+    return one_hot(iota((32, 2048), 0) == tap)
 
 
 def closure_body(
     counts_ref, owner_ref, fields_ref, in_weight_ref, in_bias_ref, depth_weight_ref, depth_bias_ref,
     mix_weight_ref, mix_bias_ref, out_weight_ref, out_bias_ref,
     out_ref,
-    spread, outgoing, incoming, grid_in, ones_mask, hidden, taps, taps_bias, depth, result, scatter,
+    spread, outgoing, incoming, grid_in, ones_mask, hidden, band, depth_bias, mix_bias, depth, result, scatter,
     place_slots, x_send, x_recv, y_send, y_recv, c_send, c_recv, leaving, arrived,
     send_sem, recv_sem, halo_send, halo_recv, back_send, back_recv,
 ):
@@ -186,49 +228,67 @@
     along_z = lane & 15
     keep_low = jnp.where(gx > 0, 1.0, 0.0).astype(F32)
     keep_high = jnp.where(gx < N_GX - 1, 1.0, 0.0).astype(F32)
+    masks = [jnp.ones((1, LANES), F32)] * 6
+    masks[0] = jnp.where(high_x, 1.0, keep_low)
+    masks[5] = jnp.where(high_x, keep_high, 1.0)
     for x in range(6):
-        mask = jnp.ones((1, LANES), F32)
-        if x == 0:
-            mask = jnp.where(high_x, 1.0, keep_low)
-        if x == 5:
-            mask = jnp.where(high_x, keep_high, 1.0)
-        ones_mask[x] = jnp.broadcast_to(mask, (16, LANES))
-    depth_weight = depth_weight_ref[...]
-    for tap in range(27):
-        taps[tap] = jnp.broadcast_to(depth_weight[:, tap : tap + 1], (HID, LANES))
-    taps_bias[...] = jnp.broadcast_to(row_to_col(depth_bias_ref[...]), (HID, LANES))
+        ones_mask[x] = jnp.broadcast_to(masks[x], (16, LANES))
+    line = iota((16, LANES), 0)
+    ones_mask[6] = jnp.where(line < 3, 1.0, jnp.where(line < 6, masks[0], masks[5]))
     in_weight = in_weight_ref[...].astype(F32)
-    in_cols = [row_to_col(in_weight[c : c + 1, :]) for c in range(CIN)]
-    column = iota((HID, 80), 1)
-    base = jnp.zeros((HID, 80), F32)
-    for c in range(CIN):
-        base = jnp.where((column >> 4) == c, 0.5 * in_cols[c], base)
-    in_bias = 0.5 * row_to_col(in_bias_ref[...])
-    first_w = jnp.concatenate(
-        [with_bias(jnp.where((column & 15) == cell, base, 0.0), in_bias, 96) for cell in range(16)],
-        axis=0,
+    first_w = [first_weights(in_weight, in_bias_ref[...], z_halo) for z_halo in (False, True)]
+    mix_w = over_cells((0.5 * mix_weight_ref[...].astype(F32)).astype(BF16))
+    out_w = over_cells(out_weight_ref[...])
+    depth_bias[...] = repeat_rows(
+        jnp.broadcast_to(row_to_col(depth_bias_ref[...]), (HID, LANES)), 8
     )
-    mix_w = with_bias(0.5 * mix_weight_ref[...].astype(F32), 0.5 * row_to_col(mix_bias_ref[...]), 48)
-    out_w = with_bias(out_weight_ref[...].astype(F32), row_to_col(out_bias_ref[...]), 48)
-    ones_cells = jnp.ones((16, 8 * LANES), BF16)
+    mix_bias[...] = repeat_rows(
+        jnp.broadcast_to(0.5 * row_to_col(mix_bias_ref[...]), (HID, LANES)), 8
+    )
+    out_bias = repeat_rows(jnp.broadcast_to(row_to_col(out_bias_ref[...]), (COUT, LANES)), 8)
+    taps = jnp.concatenate([depth_weight_ref[...], jnp.zeros((HID, 5), F32)], axis=1).astype(BF16)
+
+    def band_rows(group, carry):
+        rows = dot(taps, tap_places(lax.div(group, 2), lax.rem(group, 2)))
+        for z in range(8):
+            start = pl.multiple_of((group * 8 + z) * HID, HID)
+            for side in range(2):
+                first = z * 256 + side * LANES
+                band[side, pl.ds(start, HID), :] = rows[:, first : first + LANES]
+        return carry
+
+    lax.fori_loop(0, 8, band_rows, 0)
+    grid_in[...] = jnp.zeros_like(grid_in)
 
     every = pltpu.make_async_copy(
         outgoing.at[pl.ds(0, NDEV - 1)], incoming.at[pl.ds(0, NDEV - 1)], recv_sem
     )
     every.wait()
+
+    def place(x, y):
+        return (y // 2) * 128 + x * 16 + (y % 2) * 8
+
+    def get(c, x, y):
+        return grid_in[c, place(x, y) : place(x, y) + 8, :]
+
+    def put(c, x, y, value):
+        grid_in[c, place(x, y) : place(x, y) + 8, :] = value
 
     bricks = dot(gather, incoming[...].reshape(ROWS, CIN * LANES))
     for c in range(CIN):
         for m in range(2):
             turned = bricks[m * LANES : (m + 1) * LANES, c * LANES : (c + 1) * LANES].T
             for p in range(2):
-                grid_in[c, pl.ds((1 + 2 * m + p) * 80 + 8, 64), :] = turned[p * 64 : (p + 1) * 64]
+                for y in range(8):
+                    first = p * 64 + y * 8
+                    put(c, 1 + 2 * m + p, 1 + y, turned[first : first + 8])
 
     for c in range(CIN):
-        x_send[0, c] = pltpu.roll(grid_in[c, pl.ds(4 * 80 + 8, 64), :], 64, 1).astype(BF16)
-        x_send[1, c] = pltpu.roll(grid_in[c, pl.ds(1 * 80 + 8, 64), :], 64, 1).astype(BF16)
-        last_y = [grid_in[c, pl.ds(x * 80 + 64, 8), :] for x in range(1, 5)]
-        first_y = [grid_in[c, pl.ds(x * 80 + 8, 8), :] for x in range(1, 5)]
+        for side, x in enumerate((4, 1)):
+            cells = jnp.concatenate([get(c, x, y) for y in range(1, 9)], axis=0)
+            x_send[side, c] = pltpu.roll(cells, 64, 1).astype(BF16)
+        last_y = [get(c, x, 8) for x in range(1, 5)]
+        first_y = [get(c, x, 1) for x in range(1, 5)]
         y_send[0, c] = pltpu.roll(jnp.concatenate(last_y, axis=0), 80, 1).astype(BF16)
         y_send[1, c] = pltpu.roll(jnp.concatenate(first_y, axis=0), 48, 1).astype(BF16)
         c_send[0, c] = pltpu.roll(last_y[3], 16, 1).astype(BF16)
@@ -257,31 +317,20 @@
         )
         copy.start()
         halo.append(copy)
-    def first_group(x, pair):
-        start = pl.multiple_of(x * 80 + pair * 16, 16)
+    def first_group(pair, tile):
+        start = pl.multiple_of(pair * 128 + tile * 16, 16)
         cells = [grid_in[c, pl.ds(start, 16), :] for c in range(CIN)]
-        stacked = jnp.concatenate(cells + [ones_mask[x]], axis=0).astype(BF16)
-        value = gelu_half(dot(first_w, stacked)).astype(BF16).astype(F32)
-        for cell in range(16):
-            y = 2 * pair + cell // 8
-            z = cell % 8
-            here = value[cell * HID : (cell + 1) * HID]
-            hidden[x, y, 1 + z] = here
-            if z == 7:
-                hidden[x, y, 0] = jnp.where(
-                    along_z == 0, pltpu.roll(here, 113, 1), pltpu.roll(here, 1, 1)
-                )
-            if z == 0:
-                hidden[x, y, 9] = jnp.where(
-                    along_z == 15, pltpu.roll(here, 15, 1), pltpu.roll(here, 127, 1)
-                )
-
-    def first_inner(x, carry):
-        for pair in range(1, 4):
-            first_group(x, pair)
+        stacked = jnp.concatenate(cells + [ones_mask[min(tile, 6)]], axis=0).astype(BF16)
+        value = gelu_half(dot(first_w[tile > 5], stacked)).astype(BF16)
+        for h in range(HID):
+            hidden[h, pl.ds(start, 16), :] = value[16 * h : 16 * h + 16]
+
+    def first_inner(pair, carry):
+        for tile in range(1, 5):
+            first_group(pair, tile)
         return carry
 
-    lax.fori_loop(1, 5, first_inner, 0)
+    lax.fori_loop(1, 4, first_inner, 0)
 
     for copy in halo:
         copy.wait()
@@ -289,8 +338,9 @@
     for c in range(CIN):
         low = jnp.where(high_x, x_send[0, c].astype(F32), keep_low * x_recv[0, c].astype(F32))
         high = jnp.where(high_x, keep_high * x_recv[1, c].astype(F32), x_send[1, c].astype(F32))
-        grid_in[c, pl.ds(8, 64), :] = low
-        grid_in[c, pl.ds(5 * 80 + 8, 64), :] = high
+        for y in range(8):
+            put(c, 0, 1 + y, low[8 * y : 8 * y + 8])
+            put(c, 5, 1 + y, high[8 * y : 8 * y + 8])
         for side in range(2):
             own = y_recv[side, c].astype(F32)
             corner_low = keep_low * c_recv[0 + side, c].astype(F32)
@@ -303,60 +353,70 @@
                     far = jnp.where(high_x, corner_high, pltpu.roll(own[0:8], 64, 1))
                 else:
                     far = own[8 * (x - 1) : 8 * x]
-                near = grid_in[c, pl.ds(x * 80 + (64 if side == 0 else 8), 8), :]
-                near = pltpu.roll(near, 16 if side == 0 else 112, 1)
-                grid_in[c, pl.ds(x * 80 + (0 if side == 0 else 72), 8), :] = jnp.where(
-                    edge_lane, far, near
-                )
-
-    def first_edge_y(x, carry):
-        first_group(x, 0)
-        first_group(x, 4)
+                near = pltpu.roll(get(c, x, 8 if side == 0 else 1), 16 if side == 0 else 112, 1)
+                put(c, x, 0 if side == 0 else 9, jnp.where(edge_lane, far, near))
+        for pair in range(5):
+            below = grid_in[c, pl.ds(pair * 128 + 7, 12, stride=8), :]
+            above = grid_in[c, pl.ds(pair * 128, 12, stride=8), :]
+            grid_in[c, pair * 128 + 96 : pair * 128 + 108, :] = jnp.where(
+                along_z == 0, pltpu.roll(below, 113, 1), pltpu.roll(below, 1, 1)
+            )
+            grid_in[c, pair * 128 + 112 : pair * 128 + 124, :] = jnp.where(
+                along_z == 15, pltpu.roll(above, 15, 1), pltpu.roll(above, 127, 1)
+            )
+
+    def first_edge_y(side, carry):
+        for tile in range(1, 5):
+            first_group(4 * side, tile)
         return carry
 
     def first_edge_x(pair, carry):
-        first_group(0, pair)
-        first_group(5, pair)
+        for tile in (0, 5, 6, 7):
+            first_group(pair, tile)
         return carry
 
-    lax.fori_loop(1, 5, first_edge_y, 0)
+    lax.fori_loop(0, 2, first_edge_y, 0)
     lax.fori_loop(0, 5, first_edge_x, 0)
 
+    def depth_part(group, carry):
+        parts = []
+        for number in range(2):
+            h = 2 * group + number
+            weight = jnp.concatenate(
+                [band[side, pl.ds(h, 64, stride=HID), :] for side in range(2)], axis=1
+            ).astype(BF16)
+            cells = [hidden[h, 128 * pair : 128 * pair + 256, :] for pair in range(4)]
+            parts.append(dot(weight, jnp.concatenate(cells, axis=1)))
+        start = pl.multiple_of(16 * group, 16)
+        bias = depth_bias[pl.ds(start, 16), :]
+        for x in range(4):
+            for y in range(8):
+                rows = slice(16 * x + 8 * (y % 2), 16 * x + 8 * (y % 2) + 8)
+                lanes = slice((y // 2) * LANES, (y // 2 + 1) * LANES)
+                both = jnp.concatenate([part[rows, lanes] for part in parts], axis=0)
+                depth[x, y, pl.ds(start, 16), :] = (both + bias).astype(BF16)
+        return carry
+
+    lax.fori_loop(0, 16, depth_part, 0)
+
     def plane(x, carry):
-        def depth_part(group, inner):
-            y = lax.div(group, 4)
-            rows = pl.ds(pl.multiple_of(8 * lax.rem(group, 4), 8), 8)
-            total = [taps_bias[rows, :]] * 8
-            for a in range(3):
-                for b in range(3):
-                    cells = [hidden[x + a, y + b, z, rows, :] for z in range(10)]
-                    for c in range(3):
-                        weight = taps[9 * a + 3 * b + c, rows, :]
-                        for z in range(8):
-                            total[z] = total[z] + weight * cells[z + c]
-            for z in range(8):
-                depth[y, z, rows, :] = total[z]
+        def mix_part(group, inner):
+            for number in range(4):
+                y = 4 * group + number
+                mixed = dot(mix_w, depth[x, y]) + mix_bias[...]
+                field = dot(out_w, gelu_half(mixed).astype(BF16)) + out_bias
+                for f in range(COUT):
+                    start = pl.multiple_of(f * 64 + 8 * y, 8)
+                    result[pl.ds(start, 8), :] = field[8 * f : 8 * f + 8]
             return inner
 
-        lax.fori_loop(0, 32, depth_part, 0)
-
-        def mix_part(y, inner):
-            columns = [depth[y, z].astype(BF16) for z in range(8)]
-            stacked = jnp.concatenate([jnp.concatenate(columns, axis=1), ones_cells], axis=0)
-            mixed = gelu_half(dot(mix_w, stacked)).astype(BF16)
-            field = dot(out_w, jnp.concatenate([mixed, ones_cells], axis=0))
-            for z in range(8):
-                start = pl.multiple_of(y * 64 + 8 * z, 8)
-                result[pl.ds(start, COUT), :] = field[:, z * LANES : (z + 1) * LANES]
-            return inner
-
-        lax.fori_loop(0, 8, mix_part, 0)
+        lax.fori_loop(0, 2, mix_part, 0)
 
         odd = lax.rem(x, 2)
         turned = []
         for pair in range(3):
-            first = result[pl.ds(2 * pair + odd, 64, stride=8), :]
-            second = result[pl.ds(2 * pair + 1 - odd, 64, stride=8), :]
+            first = result[pl.ds(pl.multiple_of((2 * pair + odd) * 64, 64), 64), :]
+            second = result[pl.ds(pl.multiple_of((2 * pair + 1 - odd) * 64, 64), 64), :]
             turned.append(jnp.concatenate([first, second], axis=0).T.astype(BF16))
         packed = jnp.concatenate(turned, axis=1)
         leaving[x] = dot(scatter[...], packed).reshape(NDEV, 4, 3 * LANES).astype(BF16)
@@ -414,13 +474,14 @@
             pltpu.VMEM((CIN, ROWS, LANES), F32),
             pltpu.VMEM((NDEV, 8, CIN * LANES), BF16),
             pltpu.VMEM((NDEV, 8, CIN * LANES), BF16),
-            pltpu.VMEM((CIN, 480, LANES), F32),
-            pltpu.VMEM((6, 16, LANES), F32),
-            pltpu.VMEM((6, 10, 10, HID, LANES), F32),
-            pltpu.VMEM((27, HID, LANES), F32),
-            pltpu.VMEM((HID, LANES), F32),
-            pltpu.VMEM((8, 8, HID, LANES), F32),
-            pltpu.VMEM((512, LANES), F32),
+            pltpu.VMEM((CIN, 640, LANES), F32),
+            pltpu.VMEM((7, 16, LANES), F32),
+            pltpu.VMEM((HID, 640, LANES), BF16),
+            pltpu.VMEM((2, 64 * HID, LANES), F32),
+            pltpu.VMEM((8 * HID, LANES), F32),
+            pltpu.VMEM((8 * HID, LANES), F32),
+            pltpu.VMEM((4, 8, 8 * HID, LANES), BF16),
+            pltpu.VMEM((64 * COUT, LANES), F32),
             pltpu.VMEM((2 * SLOTS, LANES), BF16),
             pltpu.VMEM((2 * CAP, 2 * SLOTS), BF16),
             pltpu.VMEM((2, CIN, 64, LANES), BF16),
@@ -439,7 +500,7 @@
             pltpu.SemaphoreType.DMA((4,)),
         ],
         compiler_params=pltpu.CompilerParams(
-            collective_id=0, has_side_effects=True, vmem_limit_bytes=60 * 1024 * 1024
+            collective_id=0, has_side_effects=True, vmem_limit_bytes=36 * 1024 * 1024
         ),
         name="closure",
     )(

time: 74.5 us -> 73.4 us (0.985)
  Pallas kernels: 71.9 us -> 64 us
  local copies, waits for them, and re-layouts: 2.42 us -> 9.02 us
    pallas_call x1, Pallas kernels: 71.9 us -> 64 us  [shards(): pl.pallas_call(closure_body, out_shape=jax.ShapeDtypeStruct((COUT, CAP, 4...]
    unnamed x1 -> x23, local copies, waits for them, and re-layouts: 2.42 us -> 9.02 us
where the time goes in v2:
time: 73.4 us; the launch traced here: 73 us
  Pallas kernels  64 us (87%)
  local copies, waits for them, and re-layouts  9.02 us (12%)
    pallas_call x1, Pallas kernels, shards(): pl.pallas_call(closure_body, out_shape=jax.ShapeDtypeStruct((COUT, CAP, 4...  64 us
    unnamed x23, local copies, waits for them, and re-layouts  9.02 us

profile of v2, /device:TPU:1, one launch (start us, length us, event | category | flops | bytes accessed | tf_op | source)
XLA Modules:
  0.0 73.0 jit_solution(16765800098178486459)
XLA Ops:
  0.0 0.0 copy-start
  0.0 1.2 %copy-done = bf16[192,5,512]{2,0,1:T(8,128)(2,1)S(1)} copy-done((bf16[192,5,512]{2,0,1:T(8,128)(2,1)S(1)}, bf16[192,5,512]{2,0,1:T(8,128)(2,1)}, u32[]{:S(2)}) %copy-start) | copy-done | bytes 983064
  1.2 0.0 copy-start.1
  1.2 0.8 %copy-done.1 = s32[8192]{0:T(1024)S(1)} copy-done((s32[8192]{0:T(1024)S(1)}, s32[8192]{0:T(1024)}, u32[]{:S(2)}) %copy-start.1) | copy-done | bytes 32792
  2.0 0.0 copy-start.2
  2.0 0.7 copy-done.2
  2.7 0.0 copy-start.3
  2.7 0.7 copy-done.3
  3.4 0.0 copy-start.4
  3.4 0.7 copy-done.4
  4.1 0.0 copy-start.5
  4.1 0.7 copy-done.5
  4.7 0.0 copy-start.6
  4.7 0.7 copy-done.6
  5.4 0.0 copy-start.7
  5.4 0.7 copy-done.7
  6.1 0.0 copy-start.8
  6.1 0.7 copy-done.8
  6.7 0.0 copy-start.9
  6.7 0.7 copy-done.9
  7.4 0.0 copy-start.10
  7.4 0.7 copy-done.10
  8.0 64.0 %closure.1 = bf16[6,192,512]{2,1,0:T(8,128)(2,1)S(1)} custom-call(s32[1,128]{1,0:T(1,128)S(1)} %bitcast.13, s32[64,128]{1,0:T(8,128)S(1)} %bitcast.11, bf16[5,192,512]{2,1,0:T(8,128)(2,1)S(1)} %bitcast.10, bf16[5,32]{1,0:T(8,128)(2,1)S(1)} %bitcast.12, f32[1,32]{1,0:T(1,128)S(1)} %bitcast.14, f32[32,27]{1,0:T(8,128)S(1)} %copy-done.2, f32[1,32]{1,0:T(1,128)S(1)} %bitcast.15, ...), custom_call_target="tpu_custom_call" | custom-call | tf_op jit(solution)/shard_map/closure/pallas_call | solution.py:468
  72.0 1.0 %copy.13 = bf16[192,6,512]{2,0,1:T(8,128)(2,1)} copy(bf16[192,6,512]{2,0,1:T(8,128)(2,1)S(1)} %bitcast.9) | data formatting | bytes 2359296
Async XLA Ops:
  0.0 1.2 %copy-start = (bf16[192,5,512]{2,0,1:T(8,128)(2,1)S(1)}, bf16[192,5,512]{2,0,1:T(8,128)(2,1)}, u32[]{:S(2)}) copy-start(bf16[192,5,512]{2,0,1:T(8,128)(2,1)} %param.11) | copy-start | bytes 2949124
  1.2 0.8 %copy-start.1 = (s32[8192]{0:T(1024)S(1)}, s32[8192]{0:T(1024)}, u32[]{:S(2)}) copy-start(s32[8192]{0:T(1024)} %param.13) | copy-start | bytes 98308
  2.0 0.7 copy-start.2
  2.7 0.7 copy-start.3
  3.4 0.7 copy-start.4
  4.1 0.7 copy-start.5
  4.7 0.7 copy-start.6
  5.4 0.7 copy-start.7
  6.1 0.7 copy-start.8
  6.7 0.7 copy-start.9
  7.4 0.7 copy-start.10

commit v3 on v2

--- a/solution.py
+++ b/solution.py
@@ -167,13 +167,27 @@
 
 
 def closure_body(
+    counts_in, owner_in, fields_in, in_weight_in, in_bias_in, depth_weight_in, depth_bias_in,
+    mix_weight_in, mix_bias_in, out_weight_in, out_bias_in,
+    out_ref,
     counts_ref, owner_ref, fields_ref, in_weight_ref, in_bias_ref, depth_weight_ref, depth_bias_ref,
-    mix_weight_ref, mix_bias_ref, out_weight_ref, out_bias_ref,
-    out_ref,
+    mix_weight_ref, mix_bias_ref, out_weight_ref, out_bias_ref, mix_w, out_w, out_bias,
     spread, outgoing, incoming, grid_in, ones_mask, hidden, band, depth_bias, mix_bias, depth, result, scatter,
     place_slots, x_send, x_recv, y_send, y_recv, c_send, c_recv, leaving, arrived,
-    send_sem, recv_sem, halo_send, halo_recv, back_send, back_recv,
+    fetch_sem, send_sem, recv_sem, halo_send, halo_recv, back_send, back_recv,
 ):
+    fetches = [
+        pltpu.make_async_copy(source, target, fetch_sem.at[number])
+        for number, (source, target) in enumerate((
+            (counts_in, counts_ref), (owner_in, owner_ref), (fields_in, fields_ref),
+            (in_weight_in, in_weight_ref), (in_bias_in, in_bias_ref),
+            (depth_weight_in, depth_weight_ref), (depth_bias_in, depth_bias_ref),
+            (mix_weight_in, mix_weight_ref), (mix_bias_in, mix_bias_ref),
+            (out_weight_in, out_weight_ref), (out_bias_in, out_bias_ref),
+        ))
+    ]
+    for fetch in fetches:
+        fetch.start()
     gx = lax.axis_index("gx")
     yz = lax.axis_index("yz")
     me = gx * N_YZ + yz
@@ -190,6 +204,8 @@
     for step in STEPS:
         pl.semaphore_signal(barrier, inc=1, device_id=coords(step)[1], device_id_type=MESH)
 
+    for fetch in fetches[:3]:
+        fetch.wait()
     counts = counts_ref[...].astype(F32)
     owner = owner_ref[...]
     key_col, key_row = slot_keys(me, counts, owner)
@@ -235,30 +251,38 @@
         ones_mask[x] = jnp.broadcast_to(masks[x], (16, LANES))
     line = iota((16, LANES), 0)
     ones_mask[6] = jnp.where(line < 3, 1.0, jnp.where(line < 6, masks[0], masks[5]))
+    for fetch in fetches[3:]:
+        fetch.wait()
     in_weight = in_weight_ref[...].astype(F32)
     first_w = [first_weights(in_weight, in_bias_ref[...], z_halo) for z_halo in (False, True)]
-    mix_w = over_cells((0.5 * mix_weight_ref[...].astype(F32)).astype(BF16))
-    out_w = over_cells(out_weight_ref[...])
+    mix_w[...] = over_cells((0.5 * mix_weight_ref[...].astype(F32)).astype(BF16))
+    out_w[...] = over_cells(out_weight_ref[...])
     depth_bias[...] = repeat_rows(
         jnp.broadcast_to(row_to_col(depth_bias_ref[...]), (HID, LANES)), 8
     )
     mix_bias[...] = repeat_rows(
         jnp.broadcast_to(0.5 * row_to_col(mix_bias_ref[...]), (HID, LANES)), 8
     )
-    out_bias = repeat_rows(jnp.broadcast_to(row_to_col(out_bias_ref[...]), (COUT, LANES)), 8)
-    taps = jnp.concatenate([depth_weight_ref[...], jnp.zeros((HID, 5), F32)], axis=1).astype(BF16)
+    out_bias[...] = repeat_rows(jnp.broadcast_to(row_to_col(out_bias_ref[...]), (COUT, LANES)), 8)
+    taps = jnp.concatenate([depth_weight_ref[...], jnp.zeros((HID, 5), F32)], axis=1)
+    high = taps.astype(BF16)
+    taps = jnp.concatenate([high, (taps - high.astype(F32)).astype(BF16)], axis=0)
 
     def band_rows(group, carry):
         rows = dot(taps, tap_places(lax.div(group, 2), lax.rem(group, 2)))
         for z in range(8):
-            start = pl.multiple_of((group * 8 + z) * HID, HID)
+            start = pl.multiple_of((group * 8 + z) * 2 * HID, 2 * HID)
             for side in range(2):
                 first = z * 256 + side * LANES
-                band[side, pl.ds(start, HID), :] = rows[:, first : first + LANES]
+                band[side, pl.ds(start, 2 * HID), :] = rows[:, first : first + LANES]
         return carry
 
     lax.fori_loop(0, 8, band_rows, 0)
     grid_in[...] = jnp.zeros_like(grid_in)
+    for pair in range(5):
+        for tile in (0, 5):
+            first = pair * 128 + tile * 16
+            hidden[:, first : first + 16, :] = jnp.zeros((HID, 16, LANES), BF16)
 
     every = pltpu.make_async_copy(
         outgoing.at[pl.ds(0, NDEV - 1)], incoming.at[pl.ds(0, NDEV - 1)], recv_sem
@@ -370,41 +394,56 @@
             first_group(4 * side, tile)
         return carry
 
-    def first_edge_x(pair, carry):
-        for tile in (0, 5, 6, 7):
+    def first_z(pair, carry):
+        for tile in (6, 7):
             first_group(pair, tile)
         return carry
 
-    lax.fori_loop(0, 2, first_edge_y, 0)
-    lax.fori_loop(0, 5, first_edge_x, 0)
-
-    def depth_part(group, carry):
-        parts = []
-        for number in range(2):
-            h = 2 * group + number
-            weight = jnp.concatenate(
-                [band[side, pl.ds(h, 64, stride=HID), :] for side in range(2)], axis=1
-            ).astype(BF16)
-            cells = [hidden[h, 128 * pair : 128 * pair + 256, :] for pair in range(4)]
-            parts.append(dot(weight, jnp.concatenate(cells, axis=1)))
-        start = pl.multiple_of(16 * group, 16)
-        bias = depth_bias[pl.ds(start, 16), :]
-        for x in range(4):
-            for y in range(8):
-                rows = slice(16 * x + 8 * (y % 2), 16 * x + 8 * (y % 2) + 8)
-                lanes = slice((y // 2) * LANES, (y // 2 + 1) * LANES)
-                both = jnp.concatenate([part[rows, lanes] for part in parts], axis=0)
-                depth[x, y, pl.ds(start, 16), :] = (both + bias).astype(BF16)
+    def first_edge_x(pair, carry):
+        for tile in (0, 5):
+            first_group(pair, tile)
         return carry
 
-    lax.fori_loop(0, 16, depth_part, 0)
+    def depth_planes(planes):
+        def depth_part(group, carry):
+            parts = []
+            for number in range(2):
+                h = 2 * group + number
+                weight = jnp.concatenate(
+                    [
+                        jnp.concatenate(
+                            [
+                                band[side, pl.ds(x * 16 * 2 * HID + part * HID + h, 16, stride=2 * HID), :]
+                                for side in range(2)
+                            ],
+                            axis=1,
+                        )
+                        for part in range(2)
+                        for x in planes
+                    ],
+                    axis=0,
+                ).astype(BF16)
+                cells = [hidden[h, 128 * pair : 128 * pair + 256, :] for pair in range(4)]
+                both = dot(weight, jnp.concatenate(cells, axis=1))
+                parts.append(both[:32] + both[32:])
+            start = pl.multiple_of(16 * group, 16)
+            bias = depth_bias[pl.ds(start, 16), :]
+            for number, x in enumerate(planes):
+                for y in range(8):
+                    first = 16 * number + 8 * (y % 2)
+                    lanes = slice((y // 2) * LANES, (y // 2 + 1) * LANES)
+                    both = jnp.concatenate([part[first : first + 8, lanes] for part in parts], axis=0)
+                    depth[x, y, pl.ds(start, 16), :] = (both + bias).astype(BF16)
+            return carry
+
+        lax.fori_loop(0, 16, depth_part, 0)
 
     def plane(x, carry):
         def mix_part(group, inner):
             for number in range(4):
                 y = 4 * group + number
-                mixed = dot(mix_w, depth[x, y]) + mix_bias[...]
-                field = dot(out_w, gelu_half(mixed).astype(BF16)) + out_bias
+                mixed = dot(mix_w[...], depth[x, y]) + mix_bias[...]
+                field = dot(out_w[...], gelu_half(mixed).astype(BF16)) + out_bias[...]
                 for f in range(COUT):
                     start = pl.multiple_of(f * 64 + 8 * y, 8)
                     result[pl.ds(start, 8), :] = field[8 * f : 8 * f + 8]
@@ -429,23 +468,29 @@
         arrived[x, me] = leaving[x, me]
         return carry
 
-    lax.fori_loop(0, 4, plane, 0)
+    lax.fori_loop(0, 2, first_edge_y, 0)
+    lax.fori_loop(0, 5, first_z, 0)
+    depth_planes((1, 2))
+    lax.fori_loop(1, 3, plane, 0)
+    lax.fori_loop(0, 5, first_edge_x, 0)
+    depth_planes((0, 3))
+    lax.fori_loop(0, 2, lambda number, carry: plane(3 * number, carry), 0)
 
     low_half = iota((1, LANES), 1) < 64
-    taken = []
-    for x in range(4):
+    taken = {}
+    for x in (1, 2, 0, 3):
         pltpu.make_async_copy(
             leaving.at[x, pl.ds(0, NDEV - 1)], arrived.at[x, pl.ds(0, NDEV - 1)], back_recv.at[x]
         ).wait()
-        taken.append(dot(place_slots[...], arrived[x].reshape(2 * SLOTS, 3 * LANES)))
-        if x % 2 == 0:
+        taken[x] = dot(place_slots[...], arrived[x].reshape(2 * SLOTS, 3 * LANES))
+        if x in (1, 2):
             continue
         for half in range(2):
             rows = slice(half * CAP, (half + 1) * CAP)
             lanes = slice((2 * half + x // 2) * LANES, (2 * half + x // 2 + 1) * LANES)
             for pair in range(3):
-                even = taken[x - 1][rows, pair * LANES : (pair + 1) * LANES]
-                odd = taken[x][rows, pair * LANES : (pair + 1) * LANES]
+                even = taken[x - x % 2][rows, pair * LANES : (pair + 1) * LANES]
+                odd = taken[x - x % 2 + 1][rows, pair * LANES : (pair + 1) * LANES]
                 out_ref[2 * pair, :, lanes] = jnp.where(low_half, even, odd).astype(BF16)
                 out_ref[2 * pair + 1, :, lanes] = pltpu.roll(
                     jnp.where(low_half, odd, even), 64, 1
@@ -459,6 +504,7 @@
 
 
 VMEM = pl.BlockSpec(memory_space=pltpu.VMEM)
+HBM = pl.BlockSpec(memory_space=pltpu.HBM)
 
 
 def shards(
@@ -468,16 +514,30 @@
     closure = pl.pallas_call(
         closure_body,
         out_shape=jax.ShapeDtypeStruct((COUT, CAP, 4 * LANES), BF16),
-        in_specs=[VMEM] * 11,
+        in_specs=[HBM] * 11,
         out_specs=VMEM,
         scratch_shapes=[
+            pltpu.VMEM((1, NDEV), I32),
+            pltpu.VMEM((64, LANES), I32),
+            pltpu.VMEM((CIN, CAP, 4 * LANES), BF16),
+            pltpu.VMEM((CIN, HID), BF16),
+            pltpu.VMEM((1, HID), F32),
+            pltpu.VMEM((HID, 27), F32),
+            pltpu.VMEM((1, HID), F32),
+            pltpu.VMEM((HID, HID), BF16),
+            pltpu.VMEM((1, HID), F32),
+            pltpu.VMEM((COUT, HID), BF16),
+            pltpu.VMEM((1, COUT), F32),
+            pltpu.VMEM((8 * HID, 8 * HID), BF16),
+            pltpu.VMEM((8 * COUT, 8 * HID), BF16),
+            pltpu.VMEM((8 * COUT, LANES), F32),
             pltpu.VMEM((CIN, ROWS, LANES), F32),
             pltpu.VMEM((NDEV, 8, CIN * LANES), BF16),
             pltpu.VMEM((NDEV, 8, CIN * LANES), BF16),
             pltpu.VMEM((CIN, 640, LANES), F32),
             pltpu.VMEM((7, 16, LANES), F32),
             pltpu.VMEM((HID, 640, LANES), BF16),
-            pltpu.VMEM((2, 64 * HID, LANES), F32),
+            pltpu.VMEM((2, 128 * HID, LANES), F32),
             pltpu.VMEM((8 * HID, LANES), F32),
             pltpu.VMEM((8 * HID, LANES), F32),
             pltpu.VMEM((4, 8, 8 * HID, LANES), BF16),
@@ -492,6 +552,7 @@
             pltpu.VMEM((4, CIN, 8, LANES), BF16),
             pltpu.VMEM((4, NDEV, 4, 3 * LANES), BF16),
             pltpu.VMEM((4, NDEV, 4, 3 * LANES), BF16),
+            pltpu.SemaphoreType.DMA((11,)),
             pltpu.SemaphoreType.DMA,
             pltpu.SemaphoreType.DMA,
             pltpu.SemaphoreType.DMA((8,)),
@@ -503,19 +564,22 @@
             collective_id=0, has_side_effects=True, vmem_limit_bytes=36 * 1024 * 1024
         ),
         name="closure",
-    )(
-        solver_counts.reshape(1, NDEV),
-        cnn_owner.reshape(64, LANES),
-        jnp.transpose(fields, (1, 0, 2)),
-        jnp.transpose(in_weight),
-        in_bias.reshape(1, HID),
-        depth_weight,
-        depth_bias.reshape(1, HID),
-        mix_weight,
-        mix_bias.reshape(1, HID),
-        out_weight,
-        out_bias.reshape(1, COUT),
-    )
+    )(*(
+        pltpu.with_memory_space_constraint(operand, pltpu.HBM)
+        for operand in (
+            solver_counts.reshape(1, NDEV),
+            cnn_owner.reshape(64, LANES),
+            jnp.transpose(fields, (1, 0, 2)),
+            jnp.transpose(in_weight),
+            in_bias.reshape(1, HID),
+            depth_weight,
+            depth_bias.reshape(1, HID),
+            mix_weight,
+            mix_bias.reshape(1, HID),
+            out_weight,
+            out_bias.reshape(1, COUT),
+        )
+    ))
     return jnp.transpose(closure, (1, 0, 2))
 
 

time: 73.4 us -> 68.6 us (0.935)
  local copies, waits for them, and re-layouts: 9.02 us -> 1.02 us
  Pallas kernels: 64 us -> 67.5 us
    unnamed x23 -> x1, local copies, waits for them, and re-layouts: 9.02 us -> 1.02 us
    pallas_call x1, Pallas kernels: 64 us -> 67.5 us  [shards(): pl.pallas_call(closure_body, out_shape=jax.ShapeDtypeStruct((COUT, CAP, 4...]
where the time goes in v3:
time: 68.6 us; the launch traced here: 68.5 us
  Pallas kernels  67.5 us (98%)
  local copies, waits for them, and re-layouts  1.02 us (1%)
    pallas_call x1, Pallas kernels, shards(): pl.pallas_call(closure_body, out_shape=jax.ShapeDtypeStruct((COUT, CAP, 4...  67.5 us

profile of v3, /device:TPU:1, one launch (start us, length us, event | category | flops | bytes accessed | tf_op | source)
XLA Modules:
  0.0 68.5 jit_solution(8869157997098452869)
XLA Ops:
  0.0 67.5 %closure.1 = bf16[6,192,512]{2,1,0:T(8,128)(2,1)S(1)} custom-call(s32[1,128]{1,0:T(1,128)} %bitcast.13, s32[64,128]{1,0:T(8,128)} %bitcast.11, bf16[5,192,512]{2,1,0:T(8,128)(2,1)} %bitcast.10, bf16[5,32]{1,0:T(8,128)(2,1)} %bitcast.12, f32[1,32]{1,0:T(1,128)} %bitcast.14, f32[32,27]{1,0:T(8,128)} %depth_weight_in.1, f32[1,32]{1,0:T(1,128)} %bitcast.15, ...), custom_call_target="tpu_custom_call" | custom-call | tf_op jit(solution)/shard_map/closure/pallas_call | solution.py:514
  67.5 1.0 %copy.13 = bf16[192,6,512]{2,0,1:T(8,128)(2,1)} copy(bf16[192,6,512]{2,0,1:T(8,128)(2,1)S(1)} %bitcast.9) | data formatting | bytes 2359296

commit v4 on v3

--- a/solution.py
+++ b/solution.py
@@ -172,7 +172,7 @@
     out_ref,
     counts_ref, owner_ref, fields_ref, in_weight_ref, in_bias_ref, depth_weight_ref, depth_bias_ref,
     mix_weight_ref, mix_bias_ref, out_weight_ref, out_bias_ref, mix_w, out_w, out_bias,
-    spread, outgoing, incoming, grid_in, ones_mask, hidden, band, depth_bias, mix_bias, depth, result, scatter,
+    spread, outgoing, incoming, grid_in, ones_mask, hidden, band, tap_w, depth_bias, mix_bias, depth, result, scatter,
     place_slots, x_send, x_recv, y_send, y_recv, c_send, c_recv, leaving, arrived,
     fetch_sem, send_sem, recv_sem, halo_send, halo_recv, back_send, back_recv,
 ):
@@ -278,6 +278,19 @@
         return carry
 
     lax.fori_loop(0, 8, band_rows, 0)
+
+    def band_channel(h, carry):
+        row = 0
+        for planes in ((1, 2), (0, 3)):
+            for part in range(2):
+                for x in planes:
+                    for side in range(2):
+                        rows = band[side, pl.ds(x * 32 * HID + part * HID + h, 16, stride=2 * HID), :]
+                        tap_w[h, row : row + 16, side * LANES : (side + 1) * LANES] = rows.astype(BF16)
+                    row += 16
+        return carry
+
+    lax.fori_loop(0, HID, band_channel, 0)
     grid_in[...] = jnp.zeros_like(grid_in)
     for pair in range(5):
         for tile in (0, 5):
@@ -409,20 +422,7 @@
             parts = []
             for number in range(2):
                 h = 2 * group + number
-                weight = jnp.concatenate(
-                    [
-                        jnp.concatenate(
-                            [
-                                band[side, pl.ds(x * 16 * 2 * HID + part * HID + h, 16, stride=2 * HID), :]
-                                for side in range(2)
-                            ],
-                            axis=1,
-                        )
-                        for part in range(2)
-                        for x in planes
-                    ],
-                    axis=0,
-                ).astype(BF16)
+                weight = tap_w[h, 64 * (planes[0] == 0) : 64 * (planes[0] == 0) + 64, :]
                 cells = [hidden[h, 128 * pair : 128 * pair + 256, :] for pair in range(4)]
                 both = dot(weight, jnp.concatenate(cells, axis=1))
                 parts.append(both[:32] + both[32:])
@@ -440,13 +440,17 @@
 
     def plane(x, carry):
         def mix_part(group, inner):
-            for number in range(4):
-                y = 4 * group + number
-                mixed = dot(mix_w[...], depth[x, y]) + mix_bias[...]
-                field = dot(out_w[...], gelu_half(mixed).astype(BF16)) + out_bias[...]
-                for f in range(COUT):
-                    start = pl.multiple_of(f * 64 + 8 * y, 8)
-                    result[pl.ds(start, 8), :] = field[8 * f : 8 * f + 8]
+            for number in range(2):
+                y = 4 * group + 2 * number
+                cells = jnp.concatenate([depth[x, y], depth[x, y + 1]], axis=1)
+                bias = jnp.concatenate([mix_bias[...]] * 2, axis=1)
+                mixed = gelu_half(dot(mix_w[...], cells) + bias).astype(BF16)
+                field = dot(out_w[...], mixed)
+                for side in range(2):
+                    part = field[:, side * LANES : (side + 1) * LANES] + out_bias[...]
+                    for f in range(COUT):
+                        start = pl.multiple_of(f * 64 + 8 * (y + side), 8)
+                        result[pl.ds(start, 8), :] = part[8 * f : 8 * f + 8]
             return inner
 
         lax.fori_loop(0, 2, mix_part, 0)
@@ -538,6 +542,7 @@
             pltpu.VMEM((7, 16, LANES), F32),
             pltpu.VMEM((HID, 640, LANES), BF16),
             pltpu.VMEM((2, 128 * HID, LANES), F32),
+            pltpu.VMEM((HID, 128, 2 * LANES), BF16),
             pltpu.VMEM((8 * HID, LANES), F32),
             pltpu.VMEM((8 * HID, LANES), F32),
             pltpu.VMEM((4, 8, 8 * HID, LANES), BF16),

time: 68.6 us -> 64.5 us (0.940)
  Pallas kernels: 67.5 us -> 63.3 us
    pallas_call x1, Pallas kernels: 67.5 us -> 63.3 us  [shards(): pl.pallas_call(closure_body, out_shape=jax.ShapeDtypeStruct((COUT, CAP, 4...]
where the time goes in v4:
time: 64.5 us; the launch traced here: 64.4 us
  Pallas kernels  63.3 us (98%)
  local copies, waits for them, and re-layouts  1.02 us (2%)
    pallas_call x1, Pallas kernels, shards(): pl.pallas_call(closure_body, out_shape=jax.ShapeDtypeStruct((COUT, CAP, 4...  63.3 us

profile of v4, /device:TPU:1, one launch (start us, length us, event | category | flops | bytes accessed | tf_op | source)
XLA Modules:
  0.0 64.4 jit_solution(16307813995004949017)
XLA Ops:
  0.0 63.3 %closure.1 = bf16[6,192,512]{2,1,0:T(8,128)(2,1)S(1)} custom-call(s32[1,128]{1,0:T(1,128)} %bitcast.13, s32[64,128]{1,0:T(8,128)} %bitcast.11, bf16[5,192,512]{2,1,0:T(8,128)(2,1)} %bitcast.10, bf16[5,32]{1,0:T(8,128)(2,1)} %bitcast.12, f32[1,32]{1,0:T(1,128)} %bitcast.14, f32[32,27]{1,0:T(8,128)} %depth_weight_in.1, f32[1,32]{1,0:T(1,128)} %bitcast.15, ...), custom_call_target="tpu_custom_call" | custom-call | tf_op jit(solution)/shard_map/closure/pallas_call | solution.py:518
  63.3 1.0 %copy.13 = bf16[192,6,512]{2,0,1:T(8,128)(2,1)} copy(bf16[192,6,512]{2,0,1:T(8,128)(2,1)S(1)} %bitcast.9) | data formatting | bytes 2359296

commit v5 on v4

--- a/solution.py
+++ b/solution.py
@@ -362,12 +362,88 @@
         for h in range(HID):
             hidden[h, pl.ds(start, 16), :] = value[16 * h : 16 * h + 16]
 
-    def first_inner(pair, carry):
-        for tile in range(1, 5):
-            first_group(pair, tile)
-        return carry
-
-    lax.fori_loop(1, 4, first_inner, 0)
+    def first_pairs(pairs, tiles):
+        def pair_tiles(number, carry):
+            for tile in tiles:
+                first_group(pairs[0] + (pairs[1] - pairs[0]) * number, tile)
+            return carry
+
+        lax.fori_loop(0, len(pairs), pair_tiles, 0)
+
+    def z_halo(pairs):
+        for c in range(CIN):
+            for pair in pairs:
+                below = grid_in[c, pl.ds(pair * 128 + 7, 12, stride=8), :]
+                above = grid_in[c, pl.ds(pair * 128, 12, stride=8), :]
+                grid_in[c, pair * 128 + 96 : pair * 128 + 108, :] = jnp.where(
+                    along_z == 0, pltpu.roll(below, 113, 1), pltpu.roll(below, 1, 1)
+                )
+                grid_in[c, pair * 128 + 112 : pair * 128 + 124, :] = jnp.where(
+                    along_z == 15, pltpu.roll(above, 15, 1), pltpu.roll(above, 127, 1)
+                )
+
+    def finish(chunk, planes, pairs):
+        tap_rows = slice(64 * (planes[0] == 0), 64 * (planes[0] == 0) + 64)
+
+        def depth_part(group, carry):
+            parts = []
+            for number in range(2):
+                h = 2 * group + number
+                cells = [hidden[h, 128 * pair : 128 * pair + 256, :] for pair in pairs]
+                both = dot(tap_w[h, tap_rows, :], jnp.concatenate(cells, axis=1))
+                parts.append(both[:32] + both[32:])
+            start = pl.multiple_of(16 * group, 16)
+            bias = depth_bias[pl.ds(start, 16), :]
+            for x in range(2):
+                for y in range(4):
+                    first = 16 * x + 8 * (y % 2)
+                    lanes = slice((y // 2) * LANES, (y // 2 + 1) * LANES)
+                    both = jnp.concatenate([part[first : first + 8, lanes] for part in parts], axis=0)
+                    depth[4 * x + y, pl.ds(start, 16), :] = (both + bias).astype(BF16)
+            return carry
+
+        lax.fori_loop(0, 16, depth_part, 0)
+
+        def mix_part(group, carry):
+            for number in range(2):
+                row = 4 * group + 2 * number
+                cells = jnp.concatenate([depth[row], depth[row + 1]], axis=1)
+                bias = jnp.concatenate([mix_bias[...]] * 2, axis=1)
+                mixed = gelu_half(dot(mix_w[...], cells) + bias).astype(BF16)
+                field = dot(out_w[...], mixed)
+                for side in range(2):
+                    part = field[:, side * LANES : (side + 1) * LANES] + out_bias[...]
+                    for f in range(COUT):
+                        start = pl.multiple_of(f * 64 + 8 * (row + side), 8)
+                        result[pl.ds(start, 8), :] = part[8 * f : 8 * f + 8]
+            return carry
+
+        lax.fori_loop(0, 2, mix_part, 0)
+
+        turned = []
+        for pair in range(3):
+            blocks = [None] * 16
+            for x, plane in enumerate(planes):
+                for y in range(4):
+                    to = 8 * (plane % 2) + 2 * pairs[y // 2] + y % 2
+                    for f in range(2):
+                        start = (2 * pair + f) * 64 + x * 32 + y * 8
+                        blocks[(to + 4 * f) % 16] = result[start : start + 8, :]
+            turned.append(jnp.concatenate(blocks, axis=0).T.astype(BF16))
+        packed = jnp.concatenate(turned, axis=1)
+        leaving[chunk] = dot(scatter[...], packed).reshape(NDEV, 4, 3 * LANES).astype(BF16)
+        for step in STEPS:
+            other, where = coords(step)
+            pltpu.make_async_remote_copy(
+                src_ref=leaving.at[chunk, other], dst_ref=arrived.at[chunk, me],
+                send_sem=back_send, recv_sem=back_recv.at[chunk], device_id=where,
+                device_id_type=MESH,
+            ).start()
+        arrived[chunk, me] = leaving[chunk, me]
+
+    z_halo((1, 2, 3))
+    first_pairs((1, 2, 3), (1, 2, 3, 4, 6, 7))
+    finish(0, (1, 2), (1, 2))
 
     for copy in halo:
         copy.wait()
@@ -392,113 +468,42 @@
                     far = own[8 * (x - 1) : 8 * x]
                 near = pltpu.roll(get(c, x, 8 if side == 0 else 1), 16 if side == 0 else 112, 1)
                 put(c, x, 0 if side == 0 else 9, jnp.where(edge_lane, far, near))
-        for pair in range(5):
-            below = grid_in[c, pl.ds(pair * 128 + 7, 12, stride=8), :]
-            above = grid_in[c, pl.ds(pair * 128, 12, stride=8), :]
-            grid_in[c, pair * 128 + 96 : pair * 128 + 108, :] = jnp.where(
-                along_z == 0, pltpu.roll(below, 113, 1), pltpu.roll(below, 1, 1)
-            )
-            grid_in[c, pair * 128 + 112 : pair * 128 + 124, :] = jnp.where(
-                along_z == 15, pltpu.roll(above, 15, 1), pltpu.roll(above, 127, 1)
-            )
-
-    def first_edge_y(side, carry):
-        for tile in range(1, 5):
-            first_group(4 * side, tile)
-        return carry
-
-    def first_z(pair, carry):
-        for tile in (6, 7):
-            first_group(pair, tile)
-        return carry
-
-    def first_edge_x(pair, carry):
-        for tile in (0, 5):
-            first_group(pair, tile)
-        return carry
-
-    def depth_planes(planes):
-        def depth_part(group, carry):
-            parts = []
-            for number in range(2):
-                h = 2 * group + number
-                weight = tap_w[h, 64 * (planes[0] == 0) : 64 * (planes[0] == 0) + 64, :]
-                cells = [hidden[h, 128 * pair : 128 * pair + 256, :] for pair in range(4)]
-                both = dot(weight, jnp.concatenate(cells, axis=1))
-                parts.append(both[:32] + both[32:])
-            start = pl.multiple_of(16 * group, 16)
-            bias = depth_bias[pl.ds(start, 16), :]
-            for number, x in enumerate(planes):
-                for y in range(8):
-                    first = 16 * number + 8 * (y % 2)
-                    lanes = slice((y // 2) * LANES, (y // 2 + 1) * LANES)
-                    both = jnp.concatenate([part[first : first + 8, lanes] for part in parts], axis=0)
-                    depth[x, y, pl.ds(start, 16), :] = (both + bias).astype(BF16)
-            return carry
-
-        lax.fori_loop(0, 16, depth_part, 0)
-
-    def plane(x, carry):
-        def mix_part(group, inner):
-            for number in range(2):
-                y = 4 * group + 2 * number
-                cells = jnp.concatenate([depth[x, y], depth[x, y + 1]], axis=1)
-                bias = jnp.concatenate([mix_bias[...]] * 2, axis=1)
-                mixed = gelu_half(dot(mix_w[...], cells) + bias).astype(BF16)
-                field = dot(out_w[...], mixed)
-                for side in range(2):
-                    part = field[:, side * LANES : (side + 1) * LANES] + out_bias[...]
-                    for f in range(COUT):
-                        start = pl.multiple_of(f * 64 + 8 * (y + side), 8)
-                        result[pl.ds(start, 8), :] = part[8 * f : 8 * f + 8]
-            return inner
-
-        lax.fori_loop(0, 2, mix_part, 0)
-
-        odd = lax.rem(x, 2)
-        turned = []
+
+    z_halo(range(5))
+    first_pairs((0, 4), (1, 2, 3, 4, 6, 7))
+    finish(1, (1, 2), (0, 3))
+    first_pairs((1, 2, 3), (0, 5, 6, 7))
+    finish(2, (0, 3), (1, 2))
+    first_pairs((0, 4), (0, 5))
+    finish(3, (0, 3), (0, 3))
+
+    low_half = iota((1, LANES), 1) < 64
+    inner_y = ((iota((1, LANES), 1) + 16) & 63) >= 32
+    taken = []
+    sides = []
+    for chunk in range(4):
+        pltpu.make_async_copy(
+            leaving.at[chunk, pl.ds(0, NDEV - 1)], arrived.at[chunk, pl.ds(0, NDEV - 1)],
+            back_recv.at[chunk],
+        ).wait()
+        taken.append(dot(place_slots[...], arrived[chunk].reshape(2 * SLOTS, 3 * LANES)))
+        if chunk % 2 == 0:
+            continue
+        inner, outer = taken[chunk - 1], taken[chunk]
+        fields = []
         for pair in range(3):
-            first = result[pl.ds(pl.multiple_of((2 * pair + odd) * 64, 64), 64), :]
-            second = result[pl.ds(pl.multiple_of((2 * pair + 1 - odd) * 64, 64), 64), :]
-            turned.append(jnp.concatenate([first, second], axis=0).T.astype(BF16))
-        packed = jnp.concatenate(turned, axis=1)
-        leaving[x] = dot(scatter[...], packed).reshape(NDEV, 4, 3 * LANES).astype(BF16)
-        for step in STEPS:
-            other, where = coords(step)
-            pltpu.make_async_remote_copy(
-                src_ref=leaving.at[x, other], dst_ref=arrived.at[x, me],
-                send_sem=back_send, recv_sem=back_recv.at[x], device_id=where, device_id_type=MESH,
-            ).start()
-        arrived[x, me] = leaving[x, me]
-        return carry
-
-    lax.fori_loop(0, 2, first_edge_y, 0)
-    lax.fori_loop(0, 5, first_z, 0)
-    depth_planes((1, 2))
-    lax.fori_loop(1, 3, plane, 0)
-    lax.fori_loop(0, 5, first_edge_x, 0)
-    depth_planes((0, 3))
-    lax.fori_loop(0, 2, lambda number, carry: plane(3 * number, carry), 0)
-
-    low_half = iota((1, LANES), 1) < 64
-    taken = {}
-    for x in (1, 2, 0, 3):
-        pltpu.make_async_copy(
-            leaving.at[x, pl.ds(0, NDEV - 1)], arrived.at[x, pl.ds(0, NDEV - 1)], back_recv.at[x]
-        ).wait()
-        taken[x] = dot(place_slots[...], arrived[x].reshape(2 * SLOTS, 3 * LANES))
-        if x in (1, 2):
-            continue
-        for half in range(2):
-            rows = slice(half * CAP, (half + 1) * CAP)
-            lanes = slice((2 * half + x // 2) * LANES, (2 * half + x // 2 + 1) * LANES)
-            for pair in range(3):
-                even = taken[x - x % 2][rows, pair * LANES : (pair + 1) * LANES]
-                odd = taken[x - x % 2 + 1][rows, pair * LANES : (pair + 1) * LANES]
-                out_ref[2 * pair, :, lanes] = jnp.where(low_half, even, odd).astype(BF16)
-                out_ref[2 * pair + 1, :, lanes] = pltpu.roll(
-                    jnp.where(low_half, odd, even), 64, 1
-                ).astype(BF16)
+            lanes = slice(pair * LANES, (pair + 1) * LANES)
+            fields.append(jnp.where(inner_y, inner[:, lanes], outer[:, lanes]))
+            fields.append(pltpu.roll(jnp.where(inner_y, outer[:, lanes], inner[:, lanes]), 96, 1))
+        sides.append(fields)
+    for half in range(2):
+        rows = slice(half * CAP, (half + 1) * CAP)
+        for f in range(COUT):
+            middle, ends = sides[0][f][rows], sides[1][f][rows]
+            lanes = slice(2 * half * LANES, (2 * half + 1) * LANES)
+            out_ref[f, :, lanes] = jnp.where(low_half, ends, middle).astype(BF16)
+            lanes = slice((2 * half + 1) * LANES, (2 * half + 2) * LANES)
+            out_ref[f, :, lanes] = jnp.where(low_half, middle, ends).astype(BF16)
     pltpu.make_async_copy(
         outgoing.at[pl.ds(0, NDEV - 1)], incoming.at[pl.ds(0, NDEV - 1)], send_sem
     ).wait()
@@ -545,7 +550,7 @@
             pltpu.VMEM((HID, 128, 2 * LANES), BF16),
             pltpu.VMEM((8 * HID, LANES), F32),
             pltpu.VMEM((8 * HID, LANES), F32),
-            pltpu.VMEM((4, 8, 8 * HID, LANES), BF16),
+            pltpu.VMEM((8, 8 * HID, LANES), BF16),
             pltpu.VMEM((64 * COUT, LANES), F32),
             pltpu.VMEM((2 * SLOTS, LANES), BF16),
             pltpu.VMEM((2 * CAP, 2 * SLOTS), BF16),

time: 64.5 us -> 63.4 us (0.983)
  Pallas kernels: 63.3 us -> 62.3 us
    pallas_call x1, Pallas kernels: 63.3 us -> 62.3 us  [shards(): pl.pallas_call(closure_body, out_shape=jax.ShapeDtypeStruct((COUT, CAP, 4...]
where the time goes in v5:
time: 63.4 us; the launch traced here: 63.3 us
  Pallas kernels  62.3 us (98%)
  local copies, waits for them, and re-layouts  1.02 us (2%)
    pallas_call x1, Pallas kernels, shards(): pl.pallas_call(closure_body, out_shape=jax.ShapeDtypeStruct((COUT, CAP, 4...  62.3 us

profile of v5, /device:TPU:1, one launch (start us, length us, event | category | flops | bytes accessed | tf_op | source)
XLA Modules:
  0.0 63.3 jit_solution(1806748320935888609)
XLA Ops:
  0.0 62.3 %closure.1 = bf16[6,192,512]{2,1,0:T(8,128)(2,1)S(1)} custom-call(s32[1,128]{1,0:T(1,128)} %bitcast.13, s32[64,128]{1,0:T(8,128)} %bitcast.11, bf16[5,192,512]{2,1,0:T(8,128)(2,1)} %bitcast.10, bf16[5,32]{1,0:T(8,128)(2,1)} %bitcast.12, f32[1,32]{1,0:T(1,128)} %bitcast.14, f32[32,27]{1,0:T(8,128)} %depth_weight_in.1, f32[1,32]{1,0:T(1,128)} %bitcast.15, ...), custom_call_target="tpu_custom_call" | custom-call | tf_op jit(solution)/shard_map/closure/pallas_call | solution.py:523
  62.3 1.0 %copy.13 = bf16[192,6,512]{2,0,1:T(8,128)(2,1)} copy(bf16[192,6,512]{2,0,1:T(8,128)(2,1)S(1)} %bitcast.9) | data formatting | bytes 2359296

commit v6 on v5

--- a/solution.py
+++ b/solution.py
@@ -132,7 +132,7 @@
     base = repeat_rows(base, 16)
     lane = iota((16 * HID, 96), 1)
     cell = iota((16 * HID, 96), 0) & 15
-    first = jnp.where(cell < 2, 83, jnp.where((cell >> 1) == 5, 86, 80)) if z_halo else 80
+    first = 83 + 3 * ((cell >> 1) & 1) if z_halo else 80
     own = jnp.where(lane < 80, cell, -1) == (lane & 15)
     keep = own | ((lane >= first) & (lane < first + 3))
     return jnp.where(keep, base, 0.0).astype(BF16)
@@ -151,17 +151,19 @@
     z = lane >> 8
     side = (lane >> 7) & 1
     row = lane & 127
-    edge = row - 96
-    far = edge & 15
     regular = row < 96
-    in_x = jnp.where(regular, row >> 4, far >> 1)
-    in_y = jnp.where(regular, (row >> 3) & 1, far & 1)
-    in_z = jnp.where(regular, row & 7, jnp.where(edge >= 16, 8, -1))
+    inner = row < 112
+    near = (row >> 1) & 3
+    far = 5 * ((row >> 1) & 1)
+    in_x = jnp.where(regular, row >> 4, jnp.where(inner, 1 + near, far))
+    in_y = jnp.where(regular, (row >> 3) & 1, row & 1)
+    above = jnp.where(inner, row & 8, 2 * (row & 4))
+    in_z = jnp.where(regular, row & 7, above + (above >> 3) - 1)
     a = in_x - x
     b = 2 * side + in_y - pair
     c = in_z - z + 1
     valid = (a >= 0) & (a <= 2) & (b >= 0) & (b <= 2) & (c >= 0) & (c <= 2)
-    valid = valid & (regular | (far < 12))
+    valid = valid & (row < 120)
     tap = jnp.where(valid, 9 * a + 3 * b + c, -1)
     return one_hot(iota((32, 2048), 0) == tap)
 
@@ -293,7 +295,7 @@
     lax.fori_loop(0, HID, band_channel, 0)
     grid_in[...] = jnp.zeros_like(grid_in)
     for pair in range(5):
-        for tile in (0, 5):
+        for tile in (0, 5, 7):
             first = pair * 128 + tile * 16
             hidden[:, first : first + 16, :] = jnp.zeros((HID, 16, LANES), BF16)
 
@@ -357,8 +359,8 @@
     def first_group(pair, tile):
         start = pl.multiple_of(pair * 128 + tile * 16, 16)
         cells = [grid_in[c, pl.ds(start, 16), :] for c in range(CIN)]
-        stacked = jnp.concatenate(cells + [ones_mask[min(tile, 6)]], axis=0).astype(BF16)
-        value = gelu_half(dot(first_w[tile > 5], stacked)).astype(BF16)
+        stacked = jnp.concatenate(cells + [ones_mask[{6: 1, 7: 6}.get(tile, tile)]], axis=0).astype(BF16)
+        value = gelu_half(dot(first_w[tile == 7], stacked)).astype(BF16)
         for h in range(HID):
             hidden[h, pl.ds(start, 16), :] = value[16 * h : 16 * h + 16]
 
@@ -370,39 +372,50 @@
 
         lax.fori_loop(0, len(pairs), pair_tiles, 0)
 
+    def z_rows(c, source, count, target):
+        for side in range(2):
+            rows = grid_in[c, pl.ds(source + 7 * (1 - side), count, stride=8), :]
+            edge_lane = along_z == 15 * side
+            wrapped = pltpu.roll(rows, 15 if side else 113, 1)
+            moved = pltpu.roll(rows, 127 if side else 1, 1)
+            first = target + (8 if count == 8 else 4) * side
+            grid_in[c, first : first + count, :] = jnp.where(edge_lane, wrapped, moved)
+
     def z_halo(pairs):
         for c in range(CIN):
             for pair in pairs:
-                below = grid_in[c, pl.ds(pair * 128 + 7, 12, stride=8), :]
-                above = grid_in[c, pl.ds(pair * 128, 12, stride=8), :]
-                grid_in[c, pair * 128 + 96 : pair * 128 + 108, :] = jnp.where(
-                    along_z == 0, pltpu.roll(below, 113, 1), pltpu.roll(below, 1, 1)
-                )
-                grid_in[c, pair * 128 + 112 : pair * 128 + 124, :] = jnp.where(
-                    along_z == 15, pltpu.roll(above, 15, 1), pltpu.roll(above, 127, 1)
-                )
+                z_rows(c, pair * 128 + 16, 8, pair * 128 + 96)
+
+    def z_halo_edge(pairs):
+        for c in range(CIN):
+            for pair in pairs:
+                z_rows(c, pair * 128, 2, pair * 128 + 112)
+                z_rows(c, pair * 128 + 80, 2, pair * 128 + 114)
 
     def finish(chunk, planes, pairs):
         tap_rows = slice(64 * (planes[0] == 0), 64 * (planes[0] == 0) + 64)
 
         def depth_part(group, carry):
-            parts = []
-            for number in range(2):
-                h = 2 * group + number
-                cells = [hidden[h, 128 * pair : 128 * pair + 256, :] for pair in pairs]
-                both = dot(tap_w[h, tap_rows, :], jnp.concatenate(cells, axis=1))
-                parts.append(both[:32] + both[32:])
-            start = pl.multiple_of(16 * group, 16)
-            bias = depth_bias[pl.ds(start, 16), :]
-            for x in range(2):
-                for y in range(4):
-                    first = 16 * x + 8 * (y % 2)
-                    lanes = slice((y // 2) * LANES, (y // 2 + 1) * LANES)
-                    both = jnp.concatenate([part[first : first + 8, lanes] for part in parts], axis=0)
-                    depth[4 * x + y, pl.ds(start, 16), :] = (both + bias).astype(BF16)
+            for half in range(2):
+                parts = []
+                for number in range(2):
+                    h = 4 * group + 2 * half + number
+                    cells = [hidden[h, 128 * pair : 128 * pair + 256, :] for pair in pairs]
+                    both = dot(tap_w[h, tap_rows, :], jnp.concatenate(cells, axis=1))
+                    parts.append(both[:32] + both[32:])
+                start = pl.multiple_of(32 * group + 16 * half, 16)
+                bias = depth_bias[pl.ds(start, 16), :]
+                for x in range(2):
+                    for y in range(4):
+                        first = 16 * x + 8 * (y % 2)
+                        lanes = slice((y // 2) * LANES, (y // 2 + 1) * LANES)
+                        both = jnp.concatenate(
+                            [part[first : first + 8, lanes] for part in parts], axis=0
+                        )
+                        depth[4 * x + y, pl.ds(start, 16), :] = (both + bias).astype(BF16)
             return carry
 
-        lax.fori_loop(0, 16, depth_part, 0)
+        lax.fori_loop(0, 8, depth_part, 0)
 
         def mix_part(group, carry):
             for number in range(2):
@@ -442,11 +455,24 @@
         arrived[chunk, me] = leaving[chunk, me]
 
     z_halo((1, 2, 3))
-    first_pairs((1, 2, 3), (1, 2, 3, 4, 6, 7))
+    first_pairs((1, 2, 3), (1, 2, 3, 4, 6))
     finish(0, (1, 2), (1, 2))
 
     for copy in halo:
         copy.wait()
+
+    def y_rows(c, x, side, far):
+        near = pltpu.roll(get(c, x, 8 if side == 0 else 1), 16 if side == 0 else 112, 1)
+        put(c, x, 9 * side, jnp.where(along_y == 3 * side, far, near))
+
+    for c in range(CIN):
+        for side in range(2):
+            own = y_recv[side, c].astype(F32)
+            for x in range(1, 5):
+                y_rows(c, x, side, own[8 * (x - 1) : 8 * x])
+    z_halo((0, 4))
+    first_pairs((0, 4), (1, 2, 3, 4, 6))
+    finish(1, (1, 2), (0, 3))
 
     for c in range(CIN):
         low = jnp.where(high_x, x_send[0, c].astype(F32), keep_low * x_recv[0, c].astype(F32))
@@ -458,23 +484,12 @@
             own = y_recv[side, c].astype(F32)
             corner_low = keep_low * c_recv[0 + side, c].astype(F32)
             corner_high = keep_high * c_recv[2 + side, c].astype(F32)
-            edge_lane = along_y == (0 if side == 0 else 3)
-            for x in range(6):
-                if x == 0:
-                    far = jnp.where(high_x, pltpu.roll(own[24:32], 64, 1), corner_low)
-                elif x == 5:
-                    far = jnp.where(high_x, corner_high, pltpu.roll(own[0:8], 64, 1))
-                else:
-                    far = own[8 * (x - 1) : 8 * x]
-                near = pltpu.roll(get(c, x, 8 if side == 0 else 1), 16 if side == 0 else 112, 1)
-                put(c, x, 0 if side == 0 else 9, jnp.where(edge_lane, far, near))
-
-    z_halo(range(5))
-    first_pairs((0, 4), (1, 2, 3, 4, 6, 7))
-    finish(1, (1, 2), (0, 3))
-    first_pairs((1, 2, 3), (0, 5, 6, 7))
+            y_rows(c, 0, side, jnp.where(high_x, pltpu.roll(own[24:32], 64, 1), corner_low))
+            y_rows(c, 5, side, jnp.where(high_x, corner_high, pltpu.roll(own[0:8], 64, 1)))
+    z_halo_edge(range(5))
+    first_pairs((1, 2, 3), (0, 5, 7))
     finish(2, (0, 3), (1, 2))
-    first_pairs((0, 4), (0, 5))
+    first_pairs((0, 4), (0, 5, 7))
     finish(3, (0, 3), (0, 3))
 
     low_half = iota((1, LANES), 1) < 64

time: 63.4 us -> 58.5 us (0.923)
  Pallas kernels: 62.3 us -> 57.4 us
    pallas_call x1, Pallas kernels: 62.3 us -> 57.4 us  [shards(): pl.pallas_call(closure_body, out_shape=jax.ShapeDtypeStruct((COUT, CAP, 4...]
where the time goes in v6:
time: 58.5 us; the launch traced here: 58.4 us
  Pallas kernels  57.4 us (98%)
  local copies, waits for them, and re-layouts  1.02 us (2%)
    pallas_call x1, Pallas kernels, shards(): pl.pallas_call(closure_body, out_shape=jax.ShapeDtypeStruct((COUT, CAP, 4...  57.4 us

profile of v6, /device:TPU:1, one launch (start us, length us, event | category | flops | bytes accessed | tf_op | source)
XLA Modules:
  0.0 58.4 jit_solution(5923264029088187707)
XLA Ops:
  0.0 57.4 %closure.1 = bf16[6,192,512]{2,1,0:T(8,128)(2,1)S(1)} custom-call(s32[1,128]{1,0:T(1,128)} %bitcast.13, s32[64,128]{1,0:T(8,128)} %bitcast.11, bf16[5,192,512]{2,1,0:T(8,128)(2,1)} %bitcast.10, bf16[5,32]{1,0:T(8,128)(2,1)} %bitcast.12, f32[1,32]{1,0:T(1,128)} %bitcast.14, f32[32,27]{1,0:T(8,128)} %depth_weight_in.1, f32[1,32]{1,0:T(1,128)} %bitcast.15, ...), custom_call_target="tpu_custom_call" | custom-call | tf_op jit(solution)/shard_map/closure/pallas_call | solution.py:538
  57.4 1.0 %copy.13 = bf16[192,6,512]{2,0,1:T(8,128)(2,1)} copy(bf16[192,6,512]{2,0,1:T(8,128)(2,1)S(1)} %bitcast.9) | data formatting | bytes 2359296

commit v7 on v6

--- a/solution.py
+++ b/solution.py
@@ -15,7 +15,6 @@
 COUT = 6
 LANES = 128
 SLOTS = 2 * NDEV
-ROWS = 4 * SLOTS
 F32 = jnp.float32
 BF16 = jnp.bfloat16
 I32 = jnp.int32
@@ -70,16 +69,13 @@
 
 def brick_keys(cum_col):
     cum_row = col_to_row(cum_col)
-    row = iota((2 * LANES, NDEV), 0)
-    patch = (row & 63).astype(F32)
-    below = cum_row <= patch
+    below = cum_row <= (iota((LANES, NDEV), 0) & 63).astype(F32)
     source = jnp.sum(jnp.where(below, 1.0, 0.0), axis=1, keepdims=True)
     before = jnp.max(jnp.where(below, cum_row, 0.0), axis=1, keepdims=True)
-    row = iota((2 * LANES, 1), 0)
+    row = iota((LANES, 1), 0)
     place = 2.0 * source + ((row & 63).astype(F32) - before)
-    key_col = 4 * place.astype(I32) + 2 * ((row >> 6) & 1) + (row >> 7)
-    patch = (iota((NDEV, LANES), 1) & 63).astype(F32)
-    below = cum_col <= patch
+    key_col = 2 * place.astype(I32) + (row >> 6)
+    below = cum_col <= (iota((NDEV, LANES), 1) & 63).astype(F32)
     source = jnp.sum(jnp.where(below, 1.0, 0.0), axis=0, keepdims=True)
     before = jnp.max(jnp.where(below, cum_col, 0.0), axis=0, keepdims=True)
     lane = iota((1, LANES), 1)
@@ -215,25 +211,29 @@
     for c in range(CIN):
         rows = dot(select, fields_ref[c])
         for part in range(4):
-            spread[c, pl.ds(part, SLOTS, stride=4), :] = rows[:, part * LANES : (part + 1) * LANES]
+            spread[c, part % 2, pl.ds(part // 2, SLOTS, stride=2), :] = (
+                rows[:, part * LANES : (part + 1) * LANES]
+            )
     for c in range(CIN):
-        outgoing[:, :, c * LANES : (c + 1) * LANES] = (
-            spread[c].reshape(NDEV, 8, LANES).astype(BF16)
-        )
+        for m in range(2):
+            outgoing[m, :, :, c * LANES : (c + 1) * LANES] = (
+                spread[c, m].reshape(NDEV, 4, LANES).astype(BF16)
+            )
 
     pl.semaphore_wait(barrier, NDEV - 1)
 
-    for step in STEPS:
-        other, where = coords(step)
-        pltpu.make_async_remote_copy(
-            src_ref=outgoing.at[other], dst_ref=incoming.at[me],
-            send_sem=send_sem, recv_sem=recv_sem, device_id=where, device_id_type=MESH,
-        ).start()
-    incoming[me] = outgoing[me]
+    for m in range(2):
+        for step in STEPS:
+            other, where = coords(step)
+            pltpu.make_async_remote_copy(
+                src_ref=outgoing.at[m, other], dst_ref=incoming.at[m, me],
+                send_sem=send_sem, recv_sem=recv_sem.at[m], device_id=where, device_id_type=MESH,
+            ).start()
+        incoming[m, me] = outgoing[m, me]
 
     cum_col = run_cumulative(me, counts, owner)
     brick_col, brick_row = brick_keys(cum_col)
-    gather = one_hot(iota((2 * LANES, ROWS), 1) == brick_col)
+    gather = one_hot(iota((LANES, 2 * SLOTS), 1) == brick_col)
     scatter[...] = one_hot(iota((2 * SLOTS, LANES), 0) == brick_row)
     for half in range(2):
         wanted = jnp.where(key_col < 0, -1, 2 * key_col + half)
@@ -299,11 +299,6 @@
             first = pair * 128 + tile * 16
             hidden[:, first : first + 16, :] = jnp.zeros((HID, 16, LANES), BF16)
 
-    every = pltpu.make_async_copy(
-        outgoing.at[pl.ds(0, NDEV - 1)], incoming.at[pl.ds(0, NDEV - 1)], recv_sem
-    )
-    every.wait()
-
     def place(x, y):
         return (y // 2) * 128 + x * 16 + (y % 2) * 8
 
@@ -313,27 +308,48 @@
     def put(c, x, y, value):
         grid_in[c, place(x, y) : place(x, y) + 8, :] = value
 
-    bricks = dot(gather, incoming[...].reshape(ROWS, CIN * LANES))
-    for c in range(CIN):
-        for m in range(2):
-            turned = bricks[m * LANES : (m + 1) * LANES, c * LANES : (c + 1) * LANES].T
+    def first_group(pair, tile):
+        start = pl.multiple_of(pair * 128 + tile * 16, 16)
+        cells = [grid_in[c, pl.ds(start, 16), :] for c in range(CIN)]
+        stacked = jnp.concatenate(cells + [ones_mask[{6: 1, 7: 6}.get(tile, tile)]], axis=0).astype(BF16)
+        value = gelu_half(dot(first_w[tile == 7], stacked)).astype(BF16)
+        for h in range(HID):
+            hidden[h, pl.ds(start, 16), :] = value[16 * h : 16 * h + 16]
+
+    def first_pairs(pairs, tiles):
+        def pair_tiles(number, carry):
+            for tile in tiles:
+                first_group(pairs[0] + (pairs[1] - pairs[0]) * number, tile)
+            return carry
+
+        lax.fori_loop(0, len(pairs), pair_tiles, 0)
+
+    for m in range(2):
+        pltpu.make_async_copy(
+            outgoing.at[m, pl.ds(0, NDEV - 1)], incoming.at[m, pl.ds(0, NDEV - 1)], recv_sem.at[m]
+        ).wait()
+        bricks = dot(gather, incoming[m].reshape(2 * SLOTS, CIN * LANES))
+        planes = (1 + 2 * m, 2 + 2 * m)
+        far_x = (1, 4)[m]
+        for c in range(CIN):
+            turned = bricks[:, c * LANES : (c + 1) * LANES].T
             for p in range(2):
                 for y in range(8):
                     first = p * 64 + y * 8
-                    put(c, 1 + 2 * m + p, 1 + y, turned[first : first + 8])
-
-    for c in range(CIN):
-        for side, x in enumerate((4, 1)):
-            cells = jnp.concatenate([get(c, x, y) for y in range(1, 9)], axis=0)
-            x_send[side, c] = pltpu.roll(cells, 64, 1).astype(BF16)
-        last_y = [get(c, x, 8) for x in range(1, 5)]
-        first_y = [get(c, x, 1) for x in range(1, 5)]
-        y_send[0, c] = pltpu.roll(jnp.concatenate(last_y, axis=0), 80, 1).astype(BF16)
-        y_send[1, c] = pltpu.roll(jnp.concatenate(first_y, axis=0), 48, 1).astype(BF16)
-        c_send[0, c] = pltpu.roll(last_y[3], 16, 1).astype(BF16)
-        c_send[1, c] = pltpu.roll(first_y[3], 112, 1).astype(BF16)
-        c_send[2, c] = pltpu.roll(last_y[0], 16, 1).astype(BF16)
-        c_send[3, c] = pltpu.roll(first_y[0], 112, 1).astype(BF16)
+                    put(c, planes[p], 1 + y, turned[first : first + 8])
+        for c in range(CIN):
+            cells = jnp.concatenate([get(c, far_x, y) for y in range(1, 9)], axis=0)
+            x_send[1 - m, c] = pltpu.roll(cells, 64, 1).astype(BF16)
+            rows = slice(16 * m, 16 * m + 16)
+            last_y = jnp.concatenate([get(c, x, 8) for x in planes], axis=0)
+            first_y = jnp.concatenate([get(c, x, 1) for x in planes], axis=0)
+            y_send[0, c, rows] = pltpu.roll(last_y, 80, 1).astype(BF16)
+            y_send[1, c, rows] = pltpu.roll(first_y, 48, 1).astype(BF16)
+            c_send[2 - 2 * m, c] = pltpu.roll(last_y[8 * m : 8 * m + 8], 16, 1).astype(BF16)
+            c_send[3 - 2 * m, c] = pltpu.roll(first_y[8 * m : 8 * m + 8], 112, 1).astype(BF16)
+        if m == 0:
+            first_pairs((1, 2, 3), planes)
+
     up_x = lax.rem(gx + 1, N_GX)
     down_x = lax.rem(gx + N_GX - 1, N_GX)
     up_y = lax.rem(yz + 1, N_YZ)
@@ -356,22 +372,6 @@
         )
         copy.start()
         halo.append(copy)
-    def first_group(pair, tile):
-        start = pl.multiple_of(pair * 128 + tile * 16, 16)
-        cells = [grid_in[c, pl.ds(start, 16), :] for c in range(CIN)]
-        stacked = jnp.concatenate(cells + [ones_mask[{6: 1, 7: 6}.get(tile, tile)]], axis=0).astype(BF16)
-        value = gelu_half(dot(first_w[tile == 7], stacked)).astype(BF16)
-        for h in range(HID):
-            hidden[h, pl.ds(start, 16), :] = value[16 * h : 16 * h + 16]
-
-    def first_pairs(pairs, tiles):
-        def pair_tiles(number, carry):
-            for tile in tiles:
-                first_group(pairs[0] + (pairs[1] - pairs[0]) * number, tile)
-            return carry
-
-        lax.fori_loop(0, len(pairs), pair_tiles, 0)
-
     def z_rows(c, source, count, target):
         for side in range(2):
             rows = grid_in[c, pl.ds(source + 7 * (1 - side), count, stride=8), :]
@@ -455,7 +455,7 @@
         arrived[chunk, me] = leaving[chunk, me]
 
     z_halo((1, 2, 3))
-    first_pairs((1, 2, 3), (1, 2, 3, 4, 6))
+    first_pairs((1, 2, 3), (3, 4, 6))
     finish(0, (1, 2), (1, 2))
 
     for copy in halo:
@@ -520,7 +520,7 @@
             lanes = slice((2 * half + 1) * LANES, (2 * half + 2) * LANES)
             out_ref[f, :, lanes] = jnp.where(low_half, middle, ends).astype(BF16)
     pltpu.make_async_copy(
-        outgoing.at[pl.ds(0, NDEV - 1)], incoming.at[pl.ds(0, NDEV - 1)], send_sem
+        outgoing.at[:, pl.ds(0, NDEV - 1)], incoming.at[:, pl.ds(0, NDEV - 1)], send_sem
     ).wait()
     pltpu.make_async_copy(
         leaving.at[:, pl.ds(0, NDEV - 1)], arrived.at[:, pl.ds(0, NDEV - 1)], back_send
@@ -555,9 +555,9 @@
             pltpu.VMEM((8 * HID, 8 * HID), BF16),
             pltpu.VMEM((8 * COUT, 8 * HID), BF16),
             pltpu.VMEM((8 * COUT, LANES), F32),
-            pltpu.VMEM((CIN, ROWS, LANES), F32),
-            pltpu.VMEM((NDEV, 8, CIN * LANES), BF16),
-            pltpu.VMEM((NDEV, 8, CIN * LANES), BF16),
+            pltpu.VMEM((CIN, 2, 2 * SLOTS, LANES), F32),
+            pltpu.VMEM((2, NDEV, 4, CIN * LANES), BF16),
+            pltpu.VMEM((2, NDEV, 4, CIN * LANES), BF16),
             pltpu.VMEM((CIN, 640, LANES), F32),
             pltpu.VMEM((7, 16, LANES), F32),
             pltpu.VMEM((HID, 640, LANES), BF16),
@@ -579,7 +579,7 @@
             pltpu.VMEM((4, NDEV, 4, 3 * LANES), BF16),
             pltpu.SemaphoreType.DMA((11,)),
             pltpu.SemaphoreType.DMA,
-            pltpu.SemaphoreType.DMA,
+            pltpu.SemaphoreType.DMA((2,)),
             pltpu.SemaphoreType.DMA((8,)),
             pltpu.SemaphoreType.DMA((8,)),
             pltpu.SemaphoreType.DMA,

time: 58.5 us -> 58.1 us (level)
  no operation moved by 1% of the time
where the time goes in v7:
time: 58.1 us; the launch traced here: 58 us
  Pallas kernels  57 us (98%)
  local copies, waits for them, and re-layouts  1.02 us (2%)
    pallas_call x1, Pallas kernels, shards(): pl.pallas_call(closure_body, out_shape=jax.ShapeDtypeStruct((COUT, CAP, 4...  57 us

profile of v7, /device:TPU:1, one launch (start us, length us, event | category | flops | bytes accessed | tf_op | source)
XLA Modules:
  0.0 58.0 jit_solution(6948010293660042348)
XLA Ops:
  0.0 57.0 %closure.1 = bf16[6,192,512]{2,1,0:T(8,128)(2,1)S(1)} custom-call(s32[1,128]{1,0:T(1,128)} %bitcast.13, s32[64,128]{1,0:T(8,128)} %bitcast.11, bf16[5,192,512]{2,1,0:T(8,128)(2,1)} %bitcast.10, bf16[5,32]{1,0:T(8,128)(2,1)} %bitcast.12, f32[1,32]{1,0:T(1,128)} %bitcast.14, f32[32,27]{1,0:T(8,128)} %depth_weight_in.1, f32[1,32]{1,0:T(1,128)} %bitcast.15, ...), custom_call_target="tpu_custom_call" | custom-call | tf_op jit(solution)/shard_map/closure/pallas_call | solution.py:538
  57.0 1.0 %copy.13 = bf16[192,6,512]{2,0,1:T(8,128)(2,1)} copy(bf16[192,6,512]{2,0,1:T(8,128)(2,1)S(1)} %bitcast.9) | data formatting | bytes 2359296

commit v8 on v7

--- a/solution.py
+++ b/solution.py
@@ -396,14 +396,14 @@
         tap_rows = slice(64 * (planes[0] == 0), 64 * (planes[0] == 0) + 64)
 
         def depth_part(group, carry):
-            for half in range(2):
+            for half in range(4):
                 parts = []
                 for number in range(2):
-                    h = 4 * group + 2 * half + number
+                    h = 8 * group + 2 * half + number
                     cells = [hidden[h, 128 * pair : 128 * pair + 256, :] for pair in pairs]
                     both = dot(tap_w[h, tap_rows, :], jnp.concatenate(cells, axis=1))
                     parts.append(both[:32] + both[32:])
-                start = pl.multiple_of(32 * group + 16 * half, 16)
+                start = pl.multiple_of(64 * group + 16 * half, 16)
                 bias = depth_bias[pl.ds(start, 16), :]
                 for x in range(2):
                     for y in range(4):
@@ -415,23 +415,18 @@
                         depth[4 * x + y, pl.ds(start, 16), :] = (both + bias).astype(BF16)
             return carry
 
-        lax.fori_loop(0, 8, depth_part, 0)
-
-        def mix_part(group, carry):
-            for number in range(2):
-                row = 4 * group + 2 * number
-                cells = jnp.concatenate([depth[row], depth[row + 1]], axis=1)
-                bias = jnp.concatenate([mix_bias[...]] * 2, axis=1)
-                mixed = gelu_half(dot(mix_w[...], cells) + bias).astype(BF16)
-                field = dot(out_w[...], mixed)
-                for side in range(2):
-                    part = field[:, side * LANES : (side + 1) * LANES] + out_bias[...]
-                    for f in range(COUT):
-                        start = pl.multiple_of(f * 64 + 8 * (row + side), 8)
-                        result[pl.ds(start, 8), :] = part[8 * f : 8 * f + 8]
-            return carry
-
-        lax.fori_loop(0, 2, mix_part, 0)
+        lax.fori_loop(0, 4, depth_part, 0)
+
+        for row in range(0, 8, 2):
+            cells = jnp.concatenate([depth[row], depth[row + 1]], axis=1)
+            bias = jnp.concatenate([mix_bias[...]] * 2, axis=1)
+            mixed = gelu_half(dot(mix_w[...], cells) + bias).astype(BF16)
+            field = dot(out_w[...], mixed)
+            for side in range(2):
+                part = field[:, side * LANES : (side + 1) * LANES] + out_bias[...]
+                for f in range(COUT):
+                    start = f * 64 + 8 * (row + side)
+                    result[start : start + 8, :] = part[8 * f : 8 * f + 8]
 
         turned = []
         for pair in range(3):

time: 58.1 us -> 55.8 us (0.960)
  Pallas kernels: 57 us -> 54.7 us
    pallas_call x1, Pallas kernels: 57 us -> 54.7 us  [shards(): pl.pallas_call(closure_body, out_shape=jax.ShapeDtypeStruct((COUT, CAP, 4...]
where the time goes in v8:
time: 55.8 us; the launch traced here: 55.7 us
  Pallas kernels  54.7 us (98%)
  local copies, waits for them, and re-layouts  1.02 us (2%)
    pallas_call x1, Pallas kernels, shards(): pl.pallas_call(closure_body, out_shape=jax.ShapeDtypeStruct((COUT, CAP, 4...  54.7 us

profile of v8, /device:TPU:1, one launch (start us, length us, event | category | flops | bytes accessed | tf_op | source)
XLA Modules:
  0.0 55.7 jit_solution(3441979227783543468)
XLA Ops:
  0.0 54.7 %closure.1 = bf16[6,192,512]{2,1,0:T(8,128)(2,1)S(1)} custom-call(s32[1,128]{1,0:T(1,128)} %bitcast.13, s32[64,128]{1,0:T(8,128)} %bitcast.11, bf16[5,192,512]{2,1,0:T(8,128)(2,1)} %bitcast.10, bf16[5,32]{1,0:T(8,128)(2,1)} %bitcast.12, f32[1,32]{1,0:T(1,128)} %bitcast.14, f32[32,27]{1,0:T(8,128)} %depth_weight_in.1, f32[1,32]{1,0:T(1,128)} %bitcast.15, ...), custom_call_target="tpu_custom_call" | custom-call | tf_op jit(solution)/shard_map/closure/pallas_call | solution.py:533
  54.7 1.0 %copy.13 = bf16[192,6,512]{2,0,1:T(8,128)(2,1)} copy(bf16[192,6,512]{2,0,1:T(8,128)(2,1)S(1)} %bitcast.9) | data formatting | bytes 2359296
